TPU v7x, 512 devices: a whole 4x8x8 slice. The times are simulated.
512 devices in a mesh: dp: 8 (over x, core), ctx: 64 (over y, z).
Axes of the slice: x: 4, y: 8, z: 8, core: 2. Of those that a mesh axis runs over, the one named last changes fastest.
Arguments:
- segment_tokens: bfloat16 [8, 16384, 1024], P('dp', 'ctx'), may hold values from -7 to 7
- upstream_grad: bfloat16 [8, 16384, 1024], P('dp', 'ctx'), may hold values from -16 to 16
- joint_weight: bfloat16 [1024, 3072], P('ctx', 'dp'), may hold values from -0.1875 to 0.1875
- output_weight: bfloat16 [1024, 1024], P('ctx', 'dp'), may hold values from -0.1875 to 0.1875
- norm_gain: bfloat16 [1024], replicated, may hold values from 0.5 to 1.5
- ancestors: int32 [8, 128, 5], P('dp', 'ctx'), may hold values from -1 to 126, as said below
- outline_depth: int32 [8, 128], P('dp'), may hold values from 0 to 5, as said below
Outputs:
- layer_output: bfloat16 [8, 16384, 1024], P('dp', 'ctx')
- input_gradient: bfloat16 [8, 16384, 1024], P('dp', 'ctx')
- weight_gradient: float32 [1024, 1024], P('dp', 'ctx')
- header_context: bfloat16 [8, 128, 1024], P('dp', 'ctx')
Inputs may be any that keep to these rules, and one draw needn't show every extreme that they name: Entry l of segment i's list is the latest earlier segment j of level l with no segment of level l or less between j and i, for l below the depth of segment i; -1 where there is no such segment or l is not below that depth. Listed entries of one row increase. Some segment of every document lists 5 ancestors. `outline_depth`: segment i of every document has level i for i below 6; every later segment has level 1 or more; the last segment has level 5, and the one before it level 4 unless it is among the first 6.
All inputs are finite; a program needn't handle non-finite values.
Results may differ from a plain program's by a relative error of at most 0.012.
The roundings to bfloat16 on the way count: a program that leaves them out, or rounds other values in their place, can miss the bound.
Values may be sent and summed in bfloat16 or wider, within the bound.
A program may use at most 64 MiB of HBM per device.

v0:
```python
import jax
import jax.numpy as jnp
from jax import lax
from jax.sharding import PartitionSpec as P

D = 1024
H = 16
HD = 64
SEG = 128


def in_order(pieces, dim):
    lengths = list(pieces.shape[1:])
    lengths[dim] *= pieces.shape[0]
    return jnp.moveaxis(pieces, 0, dim).reshape(lengths)


def gather_together(arrays, axis, dims):
    vector = jnp.concatenate([a.reshape(-1) for a in arrays])
    lines, at, gathered = (lax.all_gather(vector, axis), 0, [])
    for a, dim in zip(arrays, dims):
        pieces = lines[:, at : at + a.size].reshape(-1, *a.shape)
        gathered.append(in_order(pieces, dim))
        at += a.size
    return tuple(gathered)


def side_by_side(arrays, axis, dim, along):
    widths = [a.shape[along] for a in arrays]
    both = jnp.concatenate(arrays, axis=along)
    filled = lax.all_gather(both, axis, axis=dim, tiled=True)
    return tuple(jnp.split(filled, [sum(widths[:k]) for k in range(1, len(widths))], axis=along))


def split_up(array, dim, peers):
    lengths = array.shape
    pieces = array.reshape(*lengths[:dim], peers, lengths[dim] // peers, *lengths[dim + 1 :])
    return jnp.moveaxis(pieces, dim, 0)


def summed_on_arrival(array, axis, dim):
    pieces = split_up(array, dim, lax.axis_size(axis))
    arrived = lax.all_to_all(pieces, axis, split_axis=0, concat_axis=0, tiled=True)
    return arrived.sum(axis=0)


def copy_for_each(array, axis):
    peers = lax.axis_size(axis)
    return lax.all_to_all(
        jnp.broadcast_to(array[None], (peers, *array.shape)), axis, 0, 0, tiled=True
    )


def gathered_copies(array, axis, dim):
    return in_order(copy_for_each(array, axis), dim)


def on_device(
    segment_tokens, upstream_grad, joint_weight, output_weight, norm_gain, ancestors, outline_depth
):
    tokens_here = segment_tokens.shape[1]
    segments_here = tokens_here // SEG
    scale = HD ** (-0.5)
    inputs = segment_tokens[0]
    upstream = upstream_grad[0]
    joint_columns, output_columns = gather_together((joint_weight, output_weight), "dp", (1, 1))
    joint_full, output_full = side_by_side((joint_columns, output_columns), "ctx", 0, 1)
    joint = jnp.dot(inputs, joint_full, preferred_element_type=jnp.float32).astype(jnp.bfloat16)
    heads = joint.reshape(segments_here, SEG, 3, H, HD)
    queries = heads[:, :, 0]
    keys_all = heads[:, :, 1]
    values = heads[:, :, 2]
    scores = (
        jnp.einsum("sqhe,skhe->shqk", queries, keys_all, preferred_element_type=jnp.float32) * scale
    )
    highest = jnp.max(scores, axis=-1, keepdims=True)
    raised = jnp.exp(scores - highest)
    shares = raised / jnp.sum(raised, axis=-1, keepdims=True)
    shares_low = shares.astype(jnp.bfloat16)
    mixed = jnp.einsum("shqk,skhe->sqhe", shares_low, values, preferred_element_type=jnp.float32)
    mixed = mixed.reshape(tokens_here, D).astype(jnp.bfloat16)
    residual = inputs.astype(jnp.float32) + jnp.dot(
        mixed, output_full, preferred_element_type=jnp.float32
    )
    average = jnp.mean(residual, axis=-1, keepdims=True)
    centered = residual - average
    spread = jnp.mean(centered * centered, axis=-1, keepdims=True)
    inverse = lax.rsqrt(spread + 1e-05)
    normed = centered * inverse
    gain_wide = norm_gain.astype(jnp.float32)
    layer_output = (normed * gain_wide).astype(jnp.bfloat16)
    scaled_grad = upstream.astype(jnp.float32) * gain_wide
    residual_grad = inverse * (
        scaled_grad
        - jnp.mean(scaled_grad, axis=-1, keepdims=True)
        - normed * jnp.mean(scaled_grad * normed, axis=-1, keepdims=True)
    )
    residual_low = residual_grad.astype(jnp.bfloat16)
    row_share = lax.psum_scatter(
        lax.dot_general(
            mixed, residual_low, (((0,), (0,)), ((), ())), preferred_element_type=jnp.float32
        ).astype(jnp.bfloat16),
        "dp",
        scatter_dimension=0,
        tiled=True,
    ).astype(jnp.float32)
    weight_gradient = summed_on_arrival(row_share, "ctx", 1)
    mixed_grad = lax.dot_general(
        residual_low, output_full, (((1,), (1,)), ((), ())), preferred_element_type=jnp.float32
    )
    mixed_grad = mixed_grad.astype(jnp.bfloat16).reshape(segments_here, SEG, H, HD)
    shares_grad = jnp.einsum(
        "sqhe,skhe->shqk", mixed_grad, values, preferred_element_type=jnp.float32
    )
    scores_grad = (
        shares * (shares_grad - jnp.sum(shares_grad * shares, axis=-1, keepdims=True)) * scale
    )
    scores_grad = scores_grad.astype(jnp.bfloat16)
    query_grad = jnp.einsum(
        "shqk,skhe->sqhe", scores_grad, keys_all, preferred_element_type=jnp.float32
    )
    key_grad = jnp.einsum(
        "shqk,sqhe->skhe", scores_grad, queries, preferred_element_type=jnp.float32
    )
    value_grad = jnp.einsum(
        "shqk,sqhe->skhe", shares_low, mixed_grad, preferred_element_type=jnp.float32
    )
    joint_grad = (
        jnp.stack([query_grad, key_grad, value_grad], axis=2)
        .reshape(tokens_here, 3 * D)
        .astype(jnp.bfloat16)
    )
    back_term = lax.dot_general(
        joint_grad, joint_full, (((1,), (1,)), ((), ())), preferred_element_type=jnp.float32
    )
    input_gradient = (residual_grad + back_term).astype(jnp.bfloat16)
    header_rows = joint.reshape(segments_here, SEG, 3 * D)[:, 0, :]
    panel = gathered_copies(header_rows[:, D:], "ctx", 0)
    total_segments = panel.shape[0]
    panel_heads = panel.reshape(total_segments, 2, H, HD)
    header_queries = header_rows[:, :D].reshape(segments_here, H, HD)
    header_scores = (
        jnp.einsum(
            "ihe,jhe->hij", header_queries, panel_heads[:, 0], preferred_element_type=jnp.float32
        )
        * scale
    )
    first_segment = lax.axis_index("ctx") * segments_here
    all_levels = outline_depth[0].astype(jnp.float32)
    own_levels = lax.dynamic_slice_in_dim(all_levels, first_segment, segments_here)
    slopes = 2.0 ** (-(jnp.arange(H, dtype=jnp.float32) + 1.0) * 4.0 / H)
    bias = -slopes[:, None, None] * (own_levels[None, :, None] - all_levels[None, None, :])
    positions = jnp.arange(total_segments, dtype=jnp.int32)
    own_positions = first_segment + jnp.arange(segments_here, dtype=jnp.int32)
    listed = jnp.any(ancestors[0][:, :, None] == positions[None, None, :], axis=1)
    kept = listed | (own_positions[:, None] == positions[None, :])
    masked = jnp.where(kept[None], header_scores + bias, -1e30)
    header_top = jnp.max(masked, axis=-1, keepdims=True)
    header_raised = jnp.exp(masked - header_top)
    header_shares = (header_raised / jnp.sum(header_raised, axis=-1, keepdims=True)).astype(
        jnp.bfloat16
    )
    context = jnp.einsum(
        "hij,jhe->ihe", header_shares, panel_heads[:, 1], preferred_element_type=jnp.float32
    )
    header_context = context.reshape(segments_here, D).astype(jnp.bfloat16)
    return (layer_output[None], input_gradient[None], weight_gradient, header_context[None])


def solution(mesh):
    return jax.shard_map(
        on_device,
        mesh=mesh,
        in_specs=(
            P("dp", "ctx", None),
            P("dp", "ctx", None),
            P("ctx", "dp"),
            P("ctx", "dp"),
            P(),
            P("dp", "ctx", None),
            P("dp", None),
        ),
        out_specs=(
            P("dp", "ctx", None),
            P("dp", "ctx", None),
            P("dp", "ctx"),
            P("dp", "ctx", None),
        ),
        check_vma=False,
    )
```

profile of v0, /device:TPU:1, one launch (start us, length us, event | category | flops | bytes accessed | tf_op | source)
XLA Modules:
  0.0 229.0 jit_solution(2289511965465113037)
XLA Ops:
  7.2 0.7 reshape.161
  7.9 0.7 pad_maximum_fusion.2
  8.6 19.4 %all-gather = bf16[65536]{0:T(1024)(128)(2,1)S(1)} all-gather(bf16[8192]{0:T(1024)(128)(2,1)S(1)} %pad_maximum_fusion.2), channel_id=2, replica_groups=mesh['dp'=8,'ctx'=64] {'dp'}, dimensions={0}, use_global_device_ids=true | all-gather | bytes 147456 | tf_op jit(solution)/shard_map/all_gather | solution.py:20
  28.2 0.7 pad_maximum_fusion.1
  28.9 0.7 convert_element_type.89
  29.6 96.8 %all-gather.3.cloned.1.call-done = bf16[1024,4096]{1,0:T(8,128)(2,1)} async-done(((bf16[16,4096]{1,0:T(8,128)(2,1)}), bf16[1024,4096]{1,0:T(8,128)(2,1)}) %all-gather.3.cloned.1.call-update) | async-done | bytes 8388624 | tf_op jit(solution)/shard_map/all_gather | solution.py:31
  126.4 6.0 %fusion.7 = bf16[3072,256]{0,1:T(8,128)(2,1)} fusion(bf16[1024,4096]{1,0:T(8,128)(2,1)} %all-gather.3.cloned.1.call-done, bf16[1,256,1024]{2,1,0:T(8,128)(2,1)} %param.7), kind=kOutput, calls=%fused_computation.7 | convolution fusion | flops 1611399168 | bytes 8388608 | tf_op jit(solution)/shard_map/dot_general | solution.py:68
  132.4 3.6 %reshape.175 = bf16[2,128,3,16,64]{4,3,2,1,0:T(8,128)(2,1)S(1)} reshape(bf16[256,3072]{1,0:T(8,128)(2,1)} %bitcast.131) | data formatting | bytes 3145728 | tf_op jit(solution)/shard_map/reshape | solution.py:69
  136.0 1.9 fusion.117
  137.9 2.1 copy.87
  140.1 2.2 copy.86
  142.3 0.9 copy.88
  143.2 2.2 fusion.120
  145.3 2.1 fusion.53
  147.4 0.5 copy.64
  148.0 2.5 %fusion.125 = (f32[256]{0:T(256)S(1)}, f32[256,1024]{1,0:T(8,128)S(1)}) fusion(bf16[1024,4096]{1,0:T(8,128)(2,1)} %all-gather.3.cloned.1.call-done, bf16[128,8,2,128]{3,2,1,0:T(2,128)(2,1)S(1)} %bitcast.129, bf16[1,256,1024]{2,1,0:T(8,128)(2,1)S(1)} %copy-done.4), kind=kOutput, calls=%fused_computation.106 | convolution fusion | flops 537657088 | bytes 4195328 | tf_op jit(solution)/shard_map/dot_general | solution.py:82
  150.5 0.3 multiply_reduce_fusion.2
  150.8 1.1 fusion.68
  151.9 2.4 %convolution_convert_fusion = bf16[1024,1024]{1,0:T(8,128)(2,1)} fusion(bf16[128,8,2,128]{3,2,1,0:T(2,128)(2,1)S(1)} %bitcast.130, f32[256,1024]{1,0:T(8,128)S(1)} %get-tuple-element.17, bf16[1,256,1024]{2,1,0:T(8,128)(2,1)S(1)} %copy-done.2, f32[256]{0:T(256)S(1)} %get-tuple-element.18, f32[256]{0:T(256)S(1)} %get-tuple-element.19, ...), kind=kOutput, calls=%fused_computation.14 | convolution fusion | flops 540278784 | bytes 4202496 | tf_op jit(solution)/shard_map/dot_general | solution.py:100
  154.3 0.6 copy-done.11
  155.0 0.1 fusion.105
  155.1 0.1 compare_or_fusion
  155.2 0.9 slice.45
  156.2 1.1 broadcast_in_dim.16
  157.3 10.0 %all-to-all-start.1 = ((bf16[64,2,2048]{2,1,0:T(2,128)(2,1)}), bf16[64,2,2048]{2,1,0:T(2,128)(2,1)S(1)}, u32[]{:S(2)}, u32[]{:S(2)}) async-start(bf16[64,2,2048]{2,1,0:T(2,128)(2,1)} %broadcast_in_dim.16), calls=%async_computation.2 | async-start | bytes 1048576 | tf_op jit(solution)/shard_map/all_to_all | solution.py:49
  167.3 3.2 %fusion.40 = bf16[256,1024]{1,0:T(8,128)(2,1)} fusion(bf16[1024,4096]{1,0:T(8,128)(2,1)} %all-gather.3.cloned.1.call-done, f32[256,1024]{1,0:T(8,128)S(1)} %get-tuple-element.17, bf16[1,256,1024]{2,1,0:T(8,128)(2,1)S(1)} %copy-done.2, f32[256]{0:T(256)S(1)} %get-tuple-element.18, f32[256]{0:T(256)S(1)} %get-tuple-element.19, ...), kind=kOutput, calls=%fused_computation.28 | convolution fusion | flops 539492352 | bytes 4202496 | tf_op jit(solution)/shard_map/dot_general | solution.py:108
  170.5 1.8 reshape.176
  172.3 1.6 copy.66
  173.9 3.0 %fusion.83 = f32[2,16,128,128]{2,3,1,0:T(8,128)} fusion(bf16[2,128,16,64]{1,3,2,0:T(8,128)(2,1)} %copy.66, bf16[2,128,1,16,64]{1,4,3,0,2:T(8,128)(2,1)S(1)} %copy.86), kind=kOutput, calls=%fused_computation.66 | convolution fusion | flops 67108864 | bytes 3145728 | tf_op jit(solution)/shard_map/sqhe,skhe->shqk/dot_general | solution.py:112
  176.9 5.1 %fusion.58 = bf16[2,128,1,16,64]{1,4,3,0,2:T(8,128)(2,1)} fusion(f32[2,16,128,128]{2,3,1,0:T(8,128)} %fusion.83, bf16[2,128,1,16,64]{1,4,3,0,2:T(8,128)(2,1)S(1)} %copy-done.8, f32[2,16,128,128]{2,3,1,0:T(8,128)} %get-tuple-element.15, f32[2,16,128]{2,1,0:T(8,128)S(1)} %get-tuple-element.14), kind=kOutput, calls=%fused_computation.36 | convolution fusion | flops 71045248 | bytes 5259264 | tf_op jit(solution)/shard_map/shqk,skhe->sqhe/dot_general | solution.py:119
  182.0 4.4 %fusion.55 = bf16[2,128,1,16,64]{1,4,3,0,2:T(8,128)(2,1)S(1)} fusion(f32[2,16,128,128]{2,3,1,0:T(8,128)} %fusion.83, bf16[2,128,1,16,64]{1,4,3,0,2:T(8,128)(2,1)S(1)} %copy-done.6, f32[2,16,128,128]{2,3,1,0:T(8,128)} %get-tuple-element.15, f32[2,16,128]{2,1,0:T(8,128)S(1)} %get-tuple-element.14), kind=kOutput, calls=%fused_computation.35 | convolution fusion | flops 71045248 | bytes 5259264 | tf_op jit(solution)/shard_map/shqk,sqhe->skhe/dot_general | solution.py:122
  186.4 2.5 %fusion.54 = bf16[2,128,1,16,64]{1,4,3,0,2:T(8,128)(2,1)S(1)} fusion(bf16[2,128,16,64]{1,3,2,0:T(8,128)(2,1)S(1)} %copy-done.1, f32[2,16,128,128]{2,3,1,0:T(8,128)} %get-tuple-element.15, f32[2,16,128]{2,1,0:T(8,128)S(1)} %get-tuple-element.14), kind=kOutput, calls=%fused_computation.34 | convolution fusion | flops 68419584 | bytes 3162112 | tf_op jit(solution)/shard_map/shqk,sqhe->skhe/dot_general | solution.py:125
  188.9 0.2 pad_maximum_fusion
  189.1 2.8 %copy.71 = bf16[2,128,3,16,64]{1,0,4,3,2:T(2,128)(2,1)} copy(bf16[2,128,3,16,64]{1,4,3,0,2:T(8,128)(2,1)S(1)} %pad_maximum_fusion) | data formatting | bytes 3145728 | tf_op jit(solution)/shard_map/stack | solution.py:129
  191.9 1.9 copy.72
  193.8 12.2 %all-to-all-start = ((f32[64,128,16]{1,2,0:T(8,128)}), f32[64,128,16]{1,2,0:T(8,128)S(1)}, u32[]{:S(2)}, u32[]{:S(2)}) async-start(f32[64,128,16]{1,2,0:T(8,128)} %bitcast.21), calls=%async_computation.1 | async-start | bytes 1048576 | tf_op jit(solution)/shard_map/all_to_all | solution.py:43
  206.0 6.1 %fusion.48 = bf16[1,256,1024]{2,1,0:T(8,128)(2,1)} fusion(bf16[1024,4096]{1,0:T(8,128)(2,1)} %all-gather.3.cloned.1.call-done, bf16[384,8,2,128]{3,2,1,0:T(2,128)(2,1)} %bitcast.133, f32[256]{0:T(256)S(1)} %get-tuple-element.18, f32[256,1024]{1,0:T(8,128)S(1)} %get-tuple-element.17, f32[256]{0:T(256)S(1)} %broadcast_multiply_fusion.2, ...), kind=kOutput, calls=%fused_computation.32 | convolution fusion | flops 1613234176 | bytes 9969664 | tf_op jit(solution)/shard_map/dot_general | solution.py:133
  212.1 0.1 reshape.171
  212.2 0.7 reshape_reshape.3
  212.9 0.2 fusion.118
  213.1 0.5 copy.91
  213.5 0.5 copy.90
  214.0 0.2 fusion.64
  214.2 0.2 fusion.126
  214.4 0.3 fusion.65
  214.7 0.7 convert_element_type.104
  215.4 6.1 %all-to-all-done = f32[64,128,16]{1,2,0:T(8,128)S(1)} async-done(((f32[64,128,16]{1,2,0:T(8,128)}), f32[64,128,16]{1,2,0:T(8,128)S(1)}, u32[]{:S(2)}, u32[]{:S(2)}) %all-to-all-start) | async-done | bytes 524320 | tf_op jit(solution)/shard_map/all_to_all | solution.py:43
  221.5 0.7 reduce_sum.78
  (46 shorter events, 0.5 us)
Async XLA Ops:
  7.2 119.2 %all-gather.3.cloned.1.call-start = ((), (), s32[]{:S(2)}) async-start(), calls=%async_computation.3 | async-start | bytes 8519680 | tf_op jit(solution)/shard_map/all_gather | solution.py:31
  28.9 163.0 %reduce-scatter.2.cloned.1.call-start = ((), (), s32[]{:S(2)}) async-start(), calls=%async_computation.4 | async-start | bytes 2359296 | tf_op jit(solution)/shard_map/reduce_scatter | solution.py:99
  137.9 4.3 %copy-start = (bf16[2,128,1,16,64]{4,3,2,1,0:T(8,128)(2,1)S(1)}, bf16[2,128,1,16,64]{4,3,2,1,0:T(8,128)(2,1)}, u32[]{:S(2)}) copy-start(bf16[2,128,1,16,64]{4,3,2,1,0:T(8,128)(2,1)} %get-tuple-element.8) | copy-start | bytes 1572868
  140.0 5.3 %copy-start.5 = (bf16[2,128,1,16,64]{1,4,3,0,2:T(8,128)(2,1)}, bf16[2,128,1,16,64]{1,4,3,0,2:T(8,128)(2,1)S(1)}, u32[]{:S(2)}) copy-start(bf16[2,128,1,16,64]{1,4,3,0,2:T(8,128)(2,1)S(1)} %copy.87) | copy-start | bytes 1572868
  143.1 4.3 %copy-start.7 = (bf16[2,128,1,16,64]{1,4,3,0,2:T(8,128)(2,1)}, bf16[2,128,1,16,64]{1,4,3,0,2:T(8,128)(2,1)S(1)}, u32[]{:S(2)}) copy-start(bf16[2,128,1,16,64]{1,4,3,0,2:T(8,128)(2,1)S(1)} %copy.88) | copy-start | bytes 1572868
  145.3 2.6 %copy-start.4 = (bf16[1,256,1024]{2,1,0:T(8,128)(2,1)S(1)}, bf16[1,256,1024]{2,1,0:T(8,128)(2,1)}, u32[]{:S(2)}) copy-start(bf16[1,256,1024]{2,1,0:T(8,128)(2,1)} %param.7) | copy-start | bytes 1572868
  148.0 2.8 %copy-start.2 = (bf16[1,256,1024]{2,1,0:T(8,128)(2,1)S(1)}, bf16[1,256,1024]{2,1,0:T(8,128)(2,1)}, u32[]{:S(2)}) copy-start(bf16[1,256,1024]{2,1,0:T(8,128)(2,1)} %param.8) | copy-start | bytes 1572868
  154.3 0.7 copy-start.11
  154.3 0.7 copy-start.10
  157.3 36.5 %all-to-all-start.1 = ((bf16[64,2,2048]{2,1,0:T(2,128)(2,1)}), bf16[64,2,2048]{2,1,0:T(2,128)(2,1)S(1)}, u32[]{:S(2)}, u32[]{:S(2)}) async-start(bf16[64,2,2048]{2,1,0:T(2,128)(2,1)} %broadcast_in_dim.16), calls=%async_computation.2 | async-start | bytes 1048576 | tf_op jit(solution)/shard_map/all_to_all | solution.py:49
  173.9 3.0 %copy-start.8 = (bf16[2,128,1,16,64]{1,4,3,0,2:T(8,128)(2,1)S(1)}, bf16[2,128,1,16,64]{1,4,3,0,2:T(8,128)(2,1)}, u32[]{:S(2)}) copy-start(bf16[2,128,1,16,64]{1,4,3,0,2:T(8,128)(2,1)} %copy-done.7) | copy-start | bytes 1572868
  176.8 5.1 %copy-start.6 = (bf16[2,128,1,16,64]{1,4,3,0,2:T(8,128)(2,1)S(1)}, bf16[2,128,1,16,64]{1,4,3,0,2:T(8,128)(2,1)}, u32[]{:S(2)}) copy-start(bf16[2,128,1,16,64]{1,4,3,0,2:T(8,128)(2,1)} %copy-done.5) | copy-start | bytes 1572868
  182.0 4.4 %copy-start.1 = (bf16[2,128,16,64]{1,3,2,0:T(8,128)(2,1)S(1)}, bf16[2,128,16,64]{1,3,2,0:T(8,128)(2,1)}, u32[]{:S(2)}) copy-start(bf16[2,128,16,64]{1,3,2,0:T(8,128)(2,1)} %copy.66) | copy-start | bytes 1572868
  186.4 2.5 %copy-start.9 = (bf16[2,128,1,16,64]{1,4,3,0,2:T(8,128)(2,1)S(1)}, bf16[2,128,1,16,64]{1,4,3,0,2:T(8,128)(2,1)}, u32[]{:S(2)}) copy-start(bf16[2,128,1,16,64]{1,4,3,0,2:T(8,128)(2,1)} %fusion.58) | copy-start | bytes 1572868
  189.1 16.9 %copy-start.3 = (bf16[1,256,1024]{2,1,0:T(8,128)(2,1)S(1)}, bf16[1,256,1024]{2,1,0:T(8,128)(2,1)}, u32[]{:S(2)}) copy-start(bf16[1,256,1024]{2,1,0:T(8,128)(2,1)} %param.8) | copy-start | bytes 1572868
  193.8 27.7 %all-to-all-start = ((f32[64,128,16]{1,2,0:T(8,128)}), f32[64,128,16]{1,2,0:T(8,128)S(1)}, u32[]{:S(2)}, u32[]{:S(2)}) async-start(f32[64,128,16]{1,2,0:T(8,128)} %bitcast.21), calls=%async_computation.1 | async-start | bytes 1048576 | tf_op jit(solution)/shard_map/all_to_all | solution.py:43
Sparse Core Ops, SparseCore 0:
  29.0 97.3 all-gather.2
  154.4 36.1 reduce-scatter.1
where the time goes:
time: 233 us; the launch traced here: 229 us
  waiting for transfers between devices  103 us (44%)
  matrix products  39.9 us (17%)
  local copies, waits for them, and re-layouts  25.5 us (11%)
  starting transfers between devices  22.2 us (10%)
  blocking collectives  19.4 us (8%)
  between operations  14.3 us (6%)
  other arithmetic  4.71 us (2%)
    all_gather x1, waiting for transfers between devices, side_by_side(): filled = lax.all_gather(both, axis, axis=dim, tiled=True)  96.8 us
    all_gather x1, blocking collectives, gather_together(): lines, at, gathered = (lax.all_gather(vector, axis), 0, [])  19.4 us
    all_to_all x1, starting transfers between devices, summed_on_arrival(): lax.all_to_all(pieces, axis, split_axis=0, concat_axis=0, tiled=True)  12.2 us
    all_to_all x1, starting transfers between devices, copy_for_each(): lax.all_to_all(jnp.broadcast_to(array[None], (peers, *array.shape)), axis...  9.98 us
    unnamed x32, local copies, waits for them, and re-layouts  6.77 us
    all_to_all x1, waiting for transfers between devices, summed_on_arrival(): lax.all_to_all(pieces, axis, split_axis=0, concat_axis=0, tiled=True)  6.13 us
    dot_general x1, matrix products, on_device(): lax.dot_general(joint_grad, joint_full, (((1,), (1,)), ((), ())), preferr...  6.11 us
    dot_general x1, matrix products, on_device(): jnp.dot(inputs, joint_full, preferred_element_type=jnp.float32)  5.96 us
  transfers between devices with their start and end apart: 4, of which 2 were waited for; matrix products, arithmetic and copies ran while one was open for 17% of the time, Pallas kernels for 0%

commit v1 on v0

v1 whole, which is shorter than its diff:
```python
import functools

import jax
import jax.numpy as jnp
from jax import lax
from jax.experimental import pallas as pl
from jax.experimental.pallas import tpu as pltpu
from jax.sharding import PartitionSpec as P

HD = 64
SEG = 128
BF = jnp.bfloat16
F32 = jnp.float32
MESH = pl.DeviceIdType.MESH
TORUS = (4, 8, 8)
NT = (((1,), (1,)), ((), ()))


def far_first(n):
    return sorted(range(1, n), key=lambda t: -min(t, n - t))


def layer_kernel(
    dims,
    x_ref,
    u_ref,
    wj_ref,
    wo_ref,
    gain_ref,
    out_ref,
    grad_ref,
    dw_ref,
    panel_ref,
    hq_ref,
    gj,
    go,
    joint,
    shares_buf,
    mixed,
    res,
    rlow,
    rlow_t,
    part,
    r0,
    a1,
    r1,
    a2,
    r2,
    a3,
    r3,
    mgrad,
    jgrad,
    hfl,
    hsend,
    ring_send,
    ring_recv,
    sems,
):
    X, Y, Z = dims
    D = x_ref.shape[1]
    pairs = D // 128
    rows = wj_ref.shape[0]
    wide = wj_ref.shape[1]
    scale = HD ** (-0.5)
    dp = lax.axis_index("dp")
    ctx = lax.axis_index("ctx")
    x, core = dp // 2, dp % 2
    y, z = ctx // Z, ctx % Z
    every = slice(None)

    def on_core(body):
        for c in (0, 1):

            @pl.when(core == c)
            def _():
                body(c)

    def send(src, dst, ssem, rsem, peer):
        pltpu.make_async_remote_copy(
            src_ref=src, dst_ref=dst, send_sem=ssem, recv_sem=rsem, device_id=peer, device_id_type=MESH
        ).start()

    def settle(ref, sem):
        pltpu.make_async_copy(ref, ref, sem).wait()

    def first_axis(c):
        return (Y, y) if c == 0 else (Z, z)

    def second_axis(c):
        return (Z, z) if c == 0 else (Y, y)

    def at_first(c, f):
        return (dp, f * Z + z) if c == 0 else (dp, y * Z + f)

    def at_second(c, s):
        return (dp, y * Z + s) if c == 0 else (dp, s * Z + z)

    def yz(c, f, s):
        return (f, s) if c == 0 else (s, f)

    def at_x(c, k):
        return (k * 2 + c, ctx)

    partner = (x * 2 + 1 - core, ctx)

    barrier = pltpu.get_barrier_semaphore()
    for t in range(1, X):
        pl.semaphore_signal(barrier, device_id=(((x + t) % X) * 2 + core, ctx), device_id_type=MESH)
    for t in range(1, Y):
        pl.semaphore_signal(barrier, device_id=(dp, ((y + t) % Y) * Z + z), device_id_type=MESH)
    for t in range(1, Z):
        pl.semaphore_signal(barrier, device_id=(dp, y * Z + (z + t) % Z), device_id_type=MESH)
    pl.semaphore_signal(barrier, device_id=partner, device_id_type=MESH)
    pl.semaphore_wait(barrier, X + Y + Z - 2)

    def gather_start(c):
        own = pltpu.make_async_copy(wj_ref, gj.at[x, c, y, z], sems.at[0])
        own_out = pltpu.make_async_copy(wo_ref, go.at[x, c, y, z], sems.at[1])
        own.start()
        own_out.start()
        for t in range(1, X):
            send(wj_ref, gj.at[x, c, y, z], sems.at[2], sems.at[3], at_x(c, (x + t) % X))
        n, f = first_axis(c)
        for t in far_first(n):
            send(wo_ref, go.at[x, c, y, z], sems.at[4], sems.at[5], at_first(c, (f + t) % n))
        own.wait()
        own_out.wait()
        if X > 1:
            settle(gj.at[pl.ds(0, X - 1), c, y, z], sems.at[3])
        for t in far_first(n):
            send(gj.at[:, c, y, z], gj.at[:, c, y, z], sems.at[6], sems.at[7], at_first(c, (f + t) % n))
        m, s = second_axis(c)
        settle(go.at[(x, c) + yz(c, pl.ds(0, n - 1), s)], sems.at[5])
        for t in far_first(m):
            ref = go.at[(x, c) + yz(c, every, s)]
            send(ref, ref, sems.at[8], sems.at[9], at_second(c, (s + t) % m))
        settle(gj.at[(every, c) + yz(c, pl.ds(0, n - 1), s)], sems.at[7])

    def carried(sign, k, j, m):
        if 2 * k < m:
            return True
        return 2 * k == m and (j < (X + 1) // 2) == (sign == 0)

    def ring(c):
        m, s = second_axis(c)

        def chunk(j, source):
            return gj.at[(j, c) + yz(c, every, source)]

        def push(sign, k, j):
            step = 1 if sign == 0 else m - 1
            ref = chunk(j, (s + (k - 1) * (m - step)) % m)
            return pltpu.make_async_remote_copy(
                src_ref=ref,
                dst_ref=ref,
                send_sem=ring_send.at[sign, k - 1, j],
                recv_sem=ring_recv.at[sign, k - 1, j],
                device_id=at_second(c, (s + step) % m),
                device_id_type=MESH,
            )

        for j in range(X):
            for sign in (0, 1):
                if carried(sign, 1, j, m):
                    push(sign, 1, j).start()
        ref = gj.at[(every, c) + yz(c, every, s)]
        send(ref, ref, sems.at[10], sems.at[11], partner)
        for k in range(1, m // 2 + 1):
            for j in range(X):
                for sign in (0, 1):
                    if not carried(sign, k, j, m):
                        continue
                    back = (m - 1) if sign == 0 else 1
                    ref = chunk(j, (s + k * back) % m)
                    settle(ref, ring_recv.at[sign, k - 1, j])
                    if carried(sign, k + 1, j, m):
                        push(sign, k + 1, j).start()
                    send(ref, ref, sems.at[10], sems.at[11], partner)
            if k == 1:
                settle(go.at[(x, c) + yz(c, every, pl.ds(0, m - 1))], sems.at[9])
                for t in range(1, X):
                    send(go.at[x, c], go.at[x, c], sems.at[12], sems.at[13], at_x(c, (x + t) % X))
        settle(gj.at[:, 1 - c], sems.at[11])

    on_core(gather_start)
    on_core(ring)

    lane = lax.broadcasted_iota(jnp.int32, (SEG, 128), 1)
    low_half = lane < HD

    def apart(pair):
        nothing = jnp.zeros_like(pair)
        return jnp.concatenate(
            [jnp.where(low_half, pair, nothing), jnp.where(low_half, nothing, pair)], axis=0
        )

    def joined(both):
        return jnp.where(low_half, both[:SEG], both[SEG:])

    def project(j, carry):
        weights = jnp.concatenate(
            [gj[j, 0].reshape(D, wide), gj[j, 1].reshape(D, wide)], axis=1
        )
        product = jnp.dot(x_ref[...], weights, preferred_element_type=F32).astype(BF)
        per = 2 * wide // 128
        for i in range(per):
            joint[per * j + i] = product[:, 128 * i : 128 * (i + 1)]
        return carry

    lax.fori_loop(0, X, project, 0)

    def hand_output_weights(c):
        if X > 1:
            settle(go.at[pl.ds(0, X - 1), c], sems.at[13])
        send(go.at[:, c], go.at[:, c], sems.at[14], sems.at[15], partner)

    on_core(hand_output_weights)

    for s in range(2):
        for g in range(pairs):
            hq_ref[s, g : g + 1, :] = joint[g, SEG * s : SEG * s + 16, :].astype(F32)[0:1]
        for g in range(2 * pairs):
            hfl[s, g : g + 1, :] = joint[pairs + g, SEG * s : SEG * s + 16, :].astype(F32)[0:1]
    hsend[...] = hfl[...].astype(BF)

    def attend(it, carry):
        p, s = it // 2, it % 2
        span = pl.ds(pl.multiple_of(s * SEG, SEG), SEG)
        queries = apart(joint[p, span, :])
        scores = lax.dot_general(queries, joint[pairs + p, span, :], NT, preferred_element_type=F32) * scale
        raised = jnp.exp(scores - jnp.max(scores, axis=-1, keepdims=True))
        shares = raised * (1.0 / jnp.sum(raised, axis=-1, keepdims=True))
        shares_buf[it] = shares
        both = jnp.dot(shares.astype(BF), joint[2 * pairs + p, span, :], preferred_element_type=F32)
        mixed[p, span, :] = joined(both).astype(BF)
        return carry

    lax.fori_loop(0, 2 * pairs, attend, 0)

    def headers_first(c):
        own = pltpu.make_async_copy(hsend, panel_ref.at[y, z], sems.at[0])
        own.start()
        n, f = first_axis(c)
        for t in far_first(n):
            send(hsend, panel_ref.at[y, z], sems.at[16], sems.at[17], at_first(c, (f + t) % n))
        own.wait()

    on_core(headers_first)

    settle_out = lambda c: settle(go.at[:, 1 - c], sems.at[15])
    on_core(settle_out)

    def mixed_all():
        return jnp.concatenate([mixed[p] for p in range(pairs)], axis=1)

    def project_out(j, carry):
        weights = jnp.concatenate([go[j, 0].reshape(D, 128), go[j, 1].reshape(D, 128)], axis=1)
        product = jnp.dot(mixed_all(), weights, preferred_element_type=F32)
        res[:, pl.ds(pl.multiple_of(j * 256, 256), 256)] = product
        return carry

    lax.fori_loop(0, X, project_out, 0)

    def headers_second(c):
        n, f = first_axis(c)
        m, s = second_axis(c)
        settle(panel_ref.at[yz(c, pl.ds(0, n - 1), s)], sems.at[17])
        for t in far_first(m):
            ref = panel_ref.at[yz(c, every, s)]
            send(ref, ref, sems.at[18], sems.at[19], at_second(c, (s + t) % m))

    on_core(headers_second)

    block = 32

    def norm(i, carry):
        span = pl.ds(pl.multiple_of(i * block, block), block)
        gain = gain_ref[...].astype(F32)
        residual = x_ref[span, :].astype(F32) + res[span, :]
        average = jnp.mean(residual, axis=-1, keepdims=True)
        centered = residual - average
        spread = jnp.mean(centered * centered, axis=-1, keepdims=True)
        inverse = lax.rsqrt(spread + 1e-05)
        normed = centered * inverse
        out_ref[span, :] = (normed * gain).astype(BF)
        scaled = u_ref[span, :].astype(F32) * gain
        first = jnp.mean(scaled, axis=-1, keepdims=True)
        second = jnp.mean(scaled * normed, axis=-1, keepdims=True)
        gradient = inverse * (scaled - first - normed * second)
        res[span, :] = gradient
        rlow[span, :] = gradient.astype(BF)
        return carry

    lax.fori_loop(0, 2 * SEG // block, norm, 0)

    for i in range(pairs):
        rlow_t[128 * i : 128 * (i + 1), :] = rlow[:, 128 * i : 128 * (i + 1)].T

    def partial_of(j, carry):
        both = jnp.concatenate([mixed[2 * j], mixed[2 * j + 1]], axis=1)
        product = jnp.dot(rlow_t[...], both, preferred_element_type=F32).astype(BF)
        part[j, 0] = product[:, :128].reshape(Y, Z, rows, 128)
        part[j, 1] = product[:, 128:].reshape(Y, Z, rows, 128)
        return carry

    lax.fori_loop(0, X, partial_of, 0)

    on_core(lambda c: send(part.at[:, 1 - c], r0, sems.at[20], sems.at[21], partner))

    tall = 2 if Y % 2 == 0 and Z * rows == 128 else 1
    height = tall * Z * rows

    def rows_of(ref, i, width):
        start = i * tall
        return jnp.concatenate(
            [
                ref[j, c, pl.ds(start, tall)].reshape(height, width)
                for j in range(X)
                for c in (0, 1)
            ],
            axis=1,
        )

    def mix_back(i, carry):
        product = lax.dot_general(rlow[...], rows_of(go, i, 128), NT, preferred_element_type=F32).astype(BF)
        for k in range(height // 128):
            mgrad[(height // 128) * i + k] = product[:, 128 * k : 128 * (k + 1)]
        return carry

    lax.fori_loop(0, Y // tall, mix_back, 0)

    settle(r0, sems.at[21])

    def pair_sum(i, carry):
        j, k = i // Y, i % Y
        a1[j, k] = (part[j, core, k].astype(F32) + r0[j, k].astype(F32)).astype(BF)
        return carry

    lax.fori_loop(0, X * Y, pair_sum, 0)

    def reduce_first(c):
        n, f = first_axis(c)
        own = pltpu.make_async_copy(a1.at[(every,) + yz(c, f, every)], r1.at[f], sems.at[0])
        own.start()
        for t in far_first(n):
            g = (f + t) % n
            send(a1.at[(every,) + yz(c, g, every)], r1.at[f], sems.at[22], sems.at[23], at_first(c, g))
        own.wait()

    on_core(reduce_first)

    def attend_back(it, carry):
        p, s = it // 2, it % 2
        span = pl.ds(pl.multiple_of(s * SEG, SEG), SEG)
        keys, values = joint[pairs + p, span, :], joint[2 * pairs + p, span, :]
        outer = apart(mgrad[p, span, :])
        shares = shares_buf[it]
        shares_grad = lax.dot_general(outer, values, NT, preferred_element_type=F32)
        inner = jnp.sum(shares_grad * shares, axis=-1, keepdims=True)
        scores_grad = (shares * (shares_grad - inner) * scale).astype(BF)
        query_grad = jnp.dot(scores_grad, keys, preferred_element_type=F32)
        jgrad[p, span, :] = joined(query_grad).astype(BF)
        key_grad = jnp.dot(scores_grad.T, apart(joint[p, span, :]), preferred_element_type=F32)
        jgrad[pairs + p, span, :] = key_grad.astype(BF)
        value_grad = jnp.dot(shares.astype(BF).T, outer, preferred_element_type=F32)
        jgrad[2 * pairs + p, span, :] = value_grad.astype(BF)
        return carry

    lax.fori_loop(0, 2 * pairs, attend_back, 0)

    def input_back(i, carry):
        left = jnp.concatenate([jgrad[g] for g in range(3 * pairs)], axis=1)
        product = lax.dot_general(left, rows_of(gj, i, wide), NT, preferred_element_type=F32)
        span = pl.ds(pl.multiple_of(i * height, height), height)
        grad_ref[:, span] = (res[:, span] + product).astype(BF)
        return carry

    lax.fori_loop(0, Y // tall, input_back, 0)

    settle(r1.at[pl.ds(0, Y - 1)], sems.at[23])

    def first_sum(i, carry):
        j = i
        total = r1[0, j].astype(F32)
        for k in range(1, Y):
            total = total + r1[k, j].astype(F32)
        a2[j] = total
        return carry

    lax.fori_loop(0, X, first_sum, 0)

    def reduce_second(c):
        m, s = second_axis(c)
        own = pltpu.make_async_copy(a2.at[:, s], r2.at[s], sems.at[0])
        own.start()
        for t in far_first(m):
            g = (s + t) % m
            send(a2.at[:, g], r2.at[s], sems.at[24], sems.at[25], at_second(c, g))
        own.wait()

    on_core(reduce_second)
    settle(r2.at[pl.ds(0, Y - 1)], sems.at[25])
    total = r2[0]
    for k in range(1, Y):
        total = total + r2[k]
    a3[...] = total

    own = pltpu.make_async_copy(a3.at[x], r3.at[x], sems.at[0])
    own.start()
    for t in range(1, X):
        k = (x + t) % X
        send(a3.at[k], r3.at[x], sems.at[26], sems.at[27], (k * 2 + core, ctx))
    own.wait()
    if X > 1:
        settle(r3.at[pl.ds(0, X - 1)], sems.at[27])
    final = r3[0]
    for k in range(1, X):
        final = final + r3[k]
    dw_ref[...] = final

    def drain(c):
        n, f = first_axis(c)
        m, s = second_axis(c)
        if X > 1:
            settle(gj.at[pl.ds(0, X - 1), c, y, z], sems.at[2])
            settle(go.at[pl.ds(0, X - 1), c], sems.at[12])
            settle(r3.at[pl.ds(0, X - 1)], sems.at[26])
        settle(go.at[(x, c) + yz(c, pl.ds(0, n - 1), s)], sems.at[4])
        settle(gj.at[(every, c) + yz(c, pl.ds(0, n - 1), s)], sems.at[6])
        settle(go.at[(x, c) + yz(c, every, pl.ds(0, m - 1))], sems.at[8])
        settle(gj.at[:, c], sems.at[10])
        settle(go.at[:, c], sems.at[14])
        settle(panel_ref.at[yz(c, pl.ds(0, n - 1), s)], sems.at[16])
        settle(panel_ref.at[yz(c, every, pl.ds(0, m - 1))], sems.at[18])
        settle(panel_ref.at[yz(c, every, pl.ds(0, m - 1))], sems.at[19])
        settle(r0, sems.at[20])
        settle(r1.at[pl.ds(0, n - 1)], sems.at[22])
        settle(r2.at[pl.ds(0, m - 1)], sems.at[24])
        for k in range(1, m // 2 + 1):
            for j in range(X):
                for sign in (0, 1):
                    if carried(sign, k, j, m):
                        settle(gj.at[(j, c) + yz(c, every, s)], ring_send.at[sign, k - 1, j])

    on_core(drain)


def call_layer(dims, tokens, upstream, joint_weight, output_weight, gain):
    X, Y, Z = dims
    T, D = tokens.shape
    pairs = D // 128
    rows, wide = joint_weight.shape
    vmem = pl.BlockSpec(memory_space=pltpu.VMEM)
    V = pltpu.VMEM
    return pl.pallas_call(
        functools.partial(layer_kernel, dims),
        out_shape=(
            jax.ShapeDtypeStruct((T, D), BF),
            jax.ShapeDtypeStruct((T, D), BF),
            jax.ShapeDtypeStruct((rows, 128), F32),
            jax.ShapeDtypeStruct((Y, Z, 2, 2 * pairs, 128), BF),
            jax.ShapeDtypeStruct((2, pairs, 128), F32),
        ),
        in_specs=[vmem] * 5,
        out_specs=(vmem,) * 5,
        scratch_shapes=[
            V((X, 2, Y, Z, rows, wide), BF),
            V((X, 2, Y, Z, rows, 128), BF),
            V((3 * pairs, T, 128), BF),
            V((2 * pairs, 2 * SEG, SEG), F32),
            V((pairs, T, 128), BF),
            V((T, D), F32),
            V((T, D), BF),
            V((D, T), BF),
            V((X, 2, Y, Z, rows, 128), BF),
            V((X, Y, Z, rows, 128), BF),
            V((X, Y, Z, rows, 128), BF),
            V((Y, X, Z, rows, 128), BF),
            V((X, Z, rows, 128), F32),
            V((Y, X, rows, 128), F32),
            V((X, rows, 128), F32),
            V((X, rows, 128), F32),
            V((pairs, T, 128), BF),
            V((3 * pairs, T, 128), BF),
            V((2, 2 * pairs, 128), F32),
            V((2, 2 * pairs, 128), BF),
            pltpu.SemaphoreType.DMA((2, max(Y // 2, 1), X)),
            pltpu.SemaphoreType.DMA((2, max(Y // 2, 1), X)),
            pltpu.SemaphoreType.DMA((28,)),
        ],
        compiler_params=pltpu.CompilerParams(collective_id=0, has_side_effects=True),
        name="segment_layer",
    )(tokens, upstream, joint_weight, output_weight, gain)


def on_device(
    dims, segment_tokens, upstream_grad, joint_weight, output_weight, norm_gain, ancestors, outline_depth
):
    T, D = segment_tokens.shape[1:]
    H = D // HD
    scale = HD ** (-0.5)
    here = T // SEG
    layer_output, input_gradient, share_t, panel, header_queries = call_layer(
        dims, segment_tokens[0], upstream_grad[0], joint_weight, output_weight, norm_gain.reshape(1, D)
    )
    weight_gradient = share_t.T
    total_segments = dims[1] * dims[2] * here
    panel_heads = panel.reshape(total_segments, 2, H, HD)
    header_queries = header_queries.reshape(here, H, HD).astype(BF)
    header_scores = (
        jnp.einsum("ihe,jhe->hij", header_queries, panel_heads[:, 0], preferred_element_type=F32) * scale
    )
    first_segment = lax.axis_index("ctx") * here
    all_levels = outline_depth[0].astype(F32)
    own_levels = lax.dynamic_slice_in_dim(all_levels, first_segment, here)
    slopes = 2.0 ** (-(jnp.arange(H, dtype=F32) + 1.0) * 4.0 / H)
    bias = -slopes[:, None, None] * (own_levels[None, :, None] - all_levels[None, None, :])
    positions = jnp.arange(total_segments, dtype=jnp.int32)
    own_positions = first_segment + jnp.arange(here, dtype=jnp.int32)
    listed = jnp.any(ancestors[0][:, :, None] == positions[None, None, :], axis=1)
    kept = listed | (own_positions[:, None] == positions[None, :])
    masked = jnp.where(kept[None], header_scores + bias, -1e30)
    header_top = jnp.max(masked, axis=-1, keepdims=True)
    header_raised = jnp.exp(masked - header_top)
    header_shares = (header_raised / jnp.sum(header_raised, axis=-1, keepdims=True)).astype(BF)
    context = jnp.einsum("hij,jhe->ihe", header_shares, panel_heads[:, 1], preferred_element_type=F32)
    header_context = context.reshape(here, D).astype(BF)
    return (layer_output[None], input_gradient[None], weight_gradient, header_context[None])


def solution(mesh, dims=TORUS):
    return jax.shard_map(
        functools.partial(on_device, dims),
        mesh=mesh,
        in_specs=(
            P("dp", "ctx", None),
            P("dp", "ctx", None),
            P("ctx", "dp"),
            P("ctx", "dp"),
            P(),
            P("dp", "ctx", None),
            P("dp", None),
        ),
        out_specs=(
            P("dp", "ctx", None),
            P("dp", "ctx", None),
            P("dp", "ctx"),
            P("dp", "ctx", None),
        ),
        check_vma=False,
    )
```

time: 233 us -> 105 us (0.45); the launches traced: 229 us -> 105 us
  waiting for transfers between devices: 103 us -> 0 us
  Pallas kernels: 0 us -> 95.4 us
  matrix products: 39.9 us -> 0.5 us
  starting transfers between devices: 22.2 us -> 0 us
  blocking collectives: 19.4 us -> 0 us
  local copies, waits for them, and re-layouts: 25.5 us -> 7.7 us
  between operations: 14.3 us -> 0.73 us
  other arithmetic: 4.71 us -> 0.44 us
    all_gather x1 -> x0, waiting for transfers between devices: 96.8 us -> none  [side_by_side(): filled = lax.all_gather(both, axis, axis=dim, tiled=True)]
    pallas_call x0 -> x1, Pallas kernels: none -> 95.4 us  [call_layer(): pl.pallas_call(functools.partial(layer_kernel, dims), out_shape=(jax.Shap...]
    dot_general x10 -> x0, matrix products: 37.2 us -> none  [the longest x1 6.11 us: on_device(): lax.dot_general(joint_grad, joint_full, (((1,), (1,)), ((), ())), preferr...]
    all_to_all x2 -> x0, starting transfers between devices: 22.2 us -> none  [the longest x1 12.2 us: summed_on_arrival(): lax.all_to_all(pieces, axis, split_axis=0, concat_axis=0, tiled=True)]
    all_gather x1 -> x0, blocking collectives: 19.4 us -> none  [gather_together(): lines, at, gathered = (lax.all_gather(vector, axis), 0, [])]
    all_to_all x2 -> x0, waiting for transfers between devices: 6.14 us -> none  [the longest x1 6.13 us: summed_on_arrival(): lax.all_to_all(pieces, axis, split_axis=0, concat_axis=0, tiled=True)]
    reshape x5 -> x2, local copies, waits for them, and re-layouts: 7.82 us -> 2.25 us  [the longest x1 1.65 us: on_device(): panel_heads = panel.reshape(total_segments, 2, H, HD)]
    another operation x2 -> x0, local copies, waits for them, and re-layouts: 3.45 us -> none  [the longest x1 2.78 us: on_device(): jnp.stack([query_grad, key_grad, value_grad], axis=2)]
  transfers between devices with their start and end apart: 4 -> 0, of which waited for: 2 -> 0; matrix products, arithmetic and copies ran while one was open for 17% -> 0% of each run, Pallas kernels for 0% -> 0%
where the time goes in v1:
time: 105 us
  Pallas kernels  95.4 us (91%)
  local copies, waits for them, and re-layouts  7.7 us (7%)
    pallas_call x1, Pallas kernels, call_layer(): pl.pallas_call(functools.partial(layer_kernel, dims), out_shape=(jax.Shap...  95.4 us
    unnamed x19, local copies, waits for them, and re-layouts  4.41 us

profile of v1, /device:TPU:1, one launch (start us, length us, event | category | flops | bytes accessed | tf_op | source)
XLA Modules:
  0.0 104.8 jit_solution(6750827578069083926)
XLA Ops:
  0.6 0.0 copy-start.4
  0.6 0.7 copy-done.4
  1.3 0.6 reshape.104.gain_ref
  1.9 95.4 %segment_layer.1 = (bf16[256,1024]{1,0:T(8,128)(2,1)}, bf16[256,1024]{1,0:T(8,128)(2,1)}, f32[16,128]{1,0:T(8,128)}, bf16[8,8,2,16,128]{4,3,2,1,0:T(8,128)(2,1)}, f32[2,8,128]{2,1,0:T(8,128)}) custom-call(bf16[256,1024]{1,0:T(8,128)(2,1)} %bitcast.22, bf16[256,1024]{1,0:T(8,128)(2,1)} %bitcast.23, bf16[16,384]{1,0:T(8,128)(2,1)} %wj_ref.1, ...), custom_call_target="tpu_custom_call" | custom-call | tf_op jit(solution)/shard_map/segment_layer/pallas_call | solution.py:455
  97.3 1.6 %reshape.105 = bf16[128,2,16,64]{3,2,1,0:T(8,128)(2,1)S(1)} reshape(bf16[8,8,2,16,128]{4,3,2,1,0:T(8,128)(2,1)} %get-tuple-element.12) | data formatting | bytes 1048576 | tf_op jit(solution)/shard_map/reshape | solution.py:508
  99.0 0.2 fusion.11
  99.2 0.5 copy.22
  99.6 0.0 copy-start.5
  99.6 0.0 copy-start.2
  99.7 0.0 copy-start.6
  99.7 0.5 copy.23
  100.1 0.0 copy-start.1
  100.1 0.2 copy-done.5
  100.3 0.1 fusion.10
  100.4 0.1 compare_or_fusion
  100.5 0.0 copy-done.2
  100.5 0.1 convert_element_type.36
  100.6 0.0 copy-done.6
  100.6 0.1 dynamic-slice_bitcast_fusion
  100.7 0.1 broadcast_subtract_fusion
  100.7 0.2 fusion.4
  100.9 0.2 fusion.13
  101.1 0.3 fusion.5
  101.4 0.7 convert_element_type.42
  102.1 0.0 copy-done.1
  102.1 0.0 copy-start
  102.1 0.8 copy.29
  102.9 0.4 copy-done
  103.4 0.0 copy-start.3
  103.4 0.8 copy.30
  104.2 0.0 copy-done.3
  104.2 0.6 copy.31
  (5 shorter events, 0.0 us)
Async XLA Ops:
  0.6 0.7 copy-start.4
  99.6 0.7 copy-start.5
  99.6 0.8 copy-start.2
  99.7 0.9 copy-start.6
  100.1 2.0 %copy-start.1 = (bf16[256,1024]{1,0:T(8,128)(2,1)S(1)}, bf16[256,1024]{1,0:T(8,128)(2,1)}, u32[]{:S(2)}) copy-start(bf16[256,1024]{1,0:T(8,128)(2,1)} %get-tuple-element.9) | copy-start | bytes 1572868
  102.1 1.2 %copy-start = (bf16[256,1024]{1,0:T(8,128)(2,1)S(1)}, bf16[256,1024]{1,0:T(8,128)(2,1)}, u32[]{:S(2)}) copy-start(bf16[256,1024]{1,0:T(8,128)(2,1)} %get-tuple-element.10) | copy-start | bytes 1572868
  103.4 0.8 copy-start.3

commit v2 on v1

v2 whole, which is shorter than its diff:
```python
import functools

import jax
import jax.numpy as jnp
from jax import lax
from jax.experimental import pallas as pl
from jax.experimental.pallas import tpu as pltpu
from jax.sharding import PartitionSpec as P

HD = 64
SEG = 128
BF = jnp.bfloat16
F32 = jnp.float32
MESH = pl.DeviceIdType.MESH
TORUS = (4, 8, 8)
NT = (((1,), (1,)), ((), ()))


def far_first(n):
    return sorted(range(1, n), key=lambda t: -min(t, n - t))


def layer_kernel(
    dims,
    tokens_ref,
    upstream_ref,
    wj_ref,
    wo_ref,
    gain_hbm,
    lists_hbm,
    depth_hbm,
    out_hbm,
    grad_hbm,
    dw_ref,
    context_ref,
    x_ref,
    u_ref,
    out_ref,
    grad_ref,
    panel,
    gj,
    go,
    joint,
    shares_buf,
    mixed,
    res,
    rlow,
    rlow_t,
    part,
    r0,
    a1,
    r1,
    tie_in,
    tie_sum,
    tie_got,
    a2,
    a2_low,
    r2,
    a3,
    r3,
    mgrad,
    jgrad,
    hq,
    hfl,
    hsend,
    wide_context,
    first_recv,
    ring_recv,
    out_recv,
    line_recv,
    gain_ref,
    lists_ref,
    depth_ref,
    sems,
):
    X, Y, Z = dims
    D = x_ref.shape[1]
    pairs = D // 128
    rows = wj_ref.shape[0]
    wide = wj_ref.shape[1]
    scale = HD ** (-0.5)
    dp = lax.axis_index("dp")
    ctx = lax.axis_index("ctx")
    x, core = dp // 2, dp % 2
    y, z = ctx // Z, ctx % Z
    every = slice(None)

    def on_core(body):
        for c in (0, 1):

            @pl.when(core == c)
            def _():
                body(c)

    def send(src, dst, ssem, rsem, peer):
        pltpu.make_async_remote_copy(
            src_ref=src, dst_ref=dst, send_sem=ssem, recv_sem=rsem, device_id=peer, device_id_type=MESH
        ).start()

    def settle(ref, sem):
        pltpu.make_async_copy(ref, ref, sem).wait()

    def first_axis(c):
        return (Y, y) if c == 0 else (Z, z)

    def second_axis(c):
        return (Z, z) if c == 0 else (Y, y)

    def at_first(c, f):
        return (dp, f * Z + z) if c == 0 else (dp, y * Z + f)

    def at_second(c, s):
        return (dp, y * Z + s) if c == 0 else (dp, s * Z + z)

    def yz(c, f, s):
        return (f, s) if c == 0 else (s, f)

    def at_x(c, k):
        return (k * 2 + c, ctx)

    partner = (x * 2 + 1 - core, ctx)

    tokens_in = pltpu.make_async_copy(tokens_ref, x_ref, sems.at[28])
    upstream_in = pltpu.make_async_copy(upstream_ref, u_ref, sems.at[29])
    tokens_in.start()
    upstream_in.start()
    small = [
        pltpu.make_async_copy(gain_hbm, gain_ref, sems.at[36]),
        pltpu.make_async_copy(lists_hbm, lists_ref, sems.at[37]),
        pltpu.make_async_copy(depth_hbm, depth_ref, sems.at[38]),
    ]
    for copy in small:
        copy.start()

    barrier = pltpu.get_barrier_semaphore()
    for t in range(1, X):
        pl.semaphore_signal(barrier, device_id=(((x + t) % X) * 2 + core, ctx), device_id_type=MESH)
    for t in range(1, Y):
        pl.semaphore_signal(barrier, device_id=(dp, ((y + t) % Y) * Z + z), device_id_type=MESH)
    for t in range(1, Z):
        pl.semaphore_signal(barrier, device_id=(dp, y * Z + (z + t) % Z), device_id_type=MESH)
    pl.semaphore_signal(barrier, device_id=partner, device_id_type=MESH)
    pl.semaphore_wait(barrier, X + Y + Z - 2)

    def gather(c):
        n, f = first_axis(c)
        m, s = second_axis(c)

        def block(o, q):
            return gj.at[(every, c) + yz(c, (f + o) % n, (s + q) % m)]

        def out_block(q):
            return go.at[(x, c) + yz(c, every, (s + q) % m)]

        def hop(ref, ssem, rsem, peer):
            send(ref, ref, ssem, rsem, peer)

        def step(sign):
            return 1 if sign == 0 else -1

        def on_second(sign, k, o):
            return 2 * k < m or (2 * k == m and (2 * o < n) == (sign == 0))

        def on_out(sign, k):
            return 2 * k < m or (2 * k == m and sign == 1)

        def push_second(sign, k, o):
            if on_second(sign, k, o):
                hop(
                    block(o, -step(sign) * (k - 1) % m),
                    sems.at[7],
                    ring_recv.at[sign, k - 1, o],
                    at_second(c, (s + step(sign) % m) % m),
                )

        def push_out(sign, k):
            if on_out(sign, k):
                hop(
                    out_block(-step(sign) * (k - 1) % m),
                    sems.at[8],
                    out_recv.at[sign, k - 1],
                    at_second(c, (s + step(sign) % m) % m),
                )

        def share(ref):
            hop(ref, sems.at[10], sems.at[11], partner)

        own = pltpu.make_async_copy(wj_ref, gj.at[x, c, y, z], sems.at[0])
        own_out = pltpu.make_async_copy(wo_ref, go.at[x, c, y, z], sems.at[1])
        own.start()
        own_out.start()
        for t in range(1, X):
            send(wj_ref, gj.at[x, c, y, z], sems.at[2], sems.at[3], at_x(c, (x + t) % X))
        near = sorted(range(1, n), key=lambda t: min(t, n - t))
        for t in near:
            send(wo_ref, go.at[x, c, y, z], sems.at[4], sems.at[5], at_first(c, (f + t) % n))
        own.wait()
        own_out.wait()
        if X > 1:
            settle(gj.at[pl.ds(0, X - 1), c, y, z], sems.at[3])
        for t in near:
            hop(block(0, 0), sems.at[6], first_recv.at[t], at_first(c, (f + t) % n))
        for sign in (0, 1):
            push_second(sign, 1, 0)
        share(block(0, 0))

        arrival = {-t % n: 1.5 + i for i, t in enumerate(near)}
        arrival[0] = 0.0
        events = [(arrival[o], 0, 0, "first", 0, o) for o in range(1, n)]
        for sign in (0, 1):
            for k in range(1, m // 2 + 1):
                for o in range(n):
                    if on_second(sign, k, o):
                        events.append((arrival[o] + 2.9 * k, 2, sign, "second", k, o))
                if on_out(sign, k):
                    events.append((3 + 2.9 * k, 1, sign, "out", k, 0))
        events.append((3, 1, 0, "plane", 0, 0))
        events.sort(key=lambda e: (e[0], e[1], -e[4], e[2]))
        left = sum(e[3] == "out" for e in events)
        for _, _, sign, kind, k, o in events:
            if kind == "first":
                settle(block(o, 0), first_recv.at[-o % n])
                for way in (0, 1):
                    push_second(way, 1, o)
                share(block(o, 0))
            elif kind == "second":
                ref = block(o, -step(sign) * k % m)
                settle(ref, ring_recv.at[sign, k - 1, o])
                push_second(sign, k + 1, o)
                share(ref)
            elif kind == "plane":
                settle(go.at[(x, c) + yz(c, pl.ds(0, n - 1), s)], sems.at[5])
                for way in (0, 1):
                    push_out(way, 1)
            else:
                settle(out_block(-step(sign) * k % m), out_recv.at[sign, k - 1])
                push_out(sign, k + 1)
                left -= 1
                if left == 0:
                    for sign in range(min(X - 1, 2)):
                        hop(go.at[x, c], sems.at[12], line_recv.at[0, sign], at_x(c, (x + step(sign)) % X))
        for sign in range(min(X - 1, 2)):
            settle(go.at[x, c], line_recv.at[0, sign])
            if X == 4:
                ref = go.at[(x - step(sign)) % X, c, pl.ds(sign * Y // 2, Y // 2)]
                hop(ref, sems.at[13], line_recv.at[1, sign], at_x(c, (x + step(sign)) % X))
        settle(gj.at[:, 1 - c], sems.at[11])

    on_core(gather)
    tokens_in.wait()

    lane = lax.broadcasted_iota(jnp.int32, (SEG, 128), 1)
    low_half = lane < HD

    def apart(pair):
        nothing = jnp.zeros_like(pair)
        return jnp.concatenate(
            [jnp.where(low_half, pair, nothing), jnp.where(low_half, nothing, pair)], axis=0
        )

    def joined(both):
        return jnp.where(low_half, both[:SEG], both[SEG:])

    def project(j, carry):
        weights = jnp.concatenate(
            [gj[j, 0].reshape(D, wide), gj[j, 1].reshape(D, wide)], axis=1
        )
        product = jnp.dot(x_ref[...], weights, preferred_element_type=F32).astype(BF)
        per = 2 * wide // 128
        for i in range(per):
            joint[per * j + i] = product[:, 128 * i : 128 * (i + 1)]
        return carry

    lax.fori_loop(0, X, project, 0)

    for s in range(2):
        for g in range(pairs):
            hq[s, g : g + 1, :] = joint[g, SEG * s : SEG * s + 16, :].astype(F32)[0:1]
        for g in range(2 * pairs):
            hfl[s, g : g + 1, :] = joint[pairs + g, SEG * s : SEG * s + 16, :].astype(F32)[0:1]
    hsend[...] = hfl[...].astype(BF)

    def headers_first(c):
        own = pltpu.make_async_copy(hsend, panel.at[y, z], sems.at[0])
        own.start()
        n, f = first_axis(c)
        for t in far_first(n):
            send(hsend, panel.at[y, z], sems.at[16], sems.at[17], at_first(c, (f + t) % n))
        own.wait()

    on_core(headers_first)

    def attend(it, carry):
        p, s = it // 2, it % 2
        span = pl.ds(pl.multiple_of(s * SEG, SEG), SEG)
        queries = apart(joint[p, span, :])
        scores = lax.dot_general(queries, joint[pairs + p, span, :], NT, preferred_element_type=F32) * scale
        raised = jnp.exp(scores - jnp.max(scores, axis=-1, keepdims=True))
        shares = raised * (1.0 / jnp.sum(raised, axis=-1, keepdims=True))
        shares_buf[it] = shares
        both = jnp.dot(shares.astype(BF), joint[2 * pairs + p, span, :], preferred_element_type=F32)
        mixed[p, span, :] = joined(both).astype(BF)
        return carry

    lax.fori_loop(0, pairs, attend, 0, unroll=4)

    def hand_output_weights(c):
        if X == 4:
            for sign in (0, 1):
                settle(go.at[x, c, pl.ds(0, Y // 2)], line_recv.at[1, sign])
        send(go.at[:, c], go.at[:, c], sems.at[14], sems.at[15], partner)

    on_core(hand_output_weights)

    lax.fori_loop(pairs, 2 * pairs, attend, 0, unroll=4)


    settle_out = lambda c: settle(go.at[:, 1 - c], sems.at[15])
    on_core(settle_out)

    def mixed_all():
        return jnp.concatenate([mixed[p] for p in range(pairs)], axis=1)

    def project_out(j, carry):
        weights = jnp.concatenate([go[j, 0].reshape(D, 128), go[j, 1].reshape(D, 128)], axis=1)
        product = jnp.dot(mixed_all(), weights, preferred_element_type=F32)
        res[:, pl.ds(pl.multiple_of(j * 256, 256), 256)] = product
        return carry

    lax.fori_loop(0, X, project_out, 0)

    def headers_second(c):
        n, f = first_axis(c)
        m, s = second_axis(c)
        settle(panel.at[yz(c, pl.ds(0, n - 1), s)], sems.at[17])
        for t in far_first(m):
            ref = panel.at[yz(c, every, s)]
            send(ref, ref, sems.at[18], sems.at[19], at_second(c, (s + t) % m))

    on_core(headers_second)
    upstream_in.wait()
    for copy in small:
        copy.wait()

    block = 32
    gain_wide = gain_ref[...].astype(F32)

    def norm(i, carry):
        span = pl.ds(pl.multiple_of(i * block, block), block)
        gain = jnp.concatenate([gain_wide[p : p + 1, :] for p in range(pairs)], axis=1)
        residual = x_ref[span, :].astype(F32) + res[span, :]
        average = jnp.mean(residual, axis=-1, keepdims=True)
        centered = residual - average
        spread = jnp.mean(centered * centered, axis=-1, keepdims=True)
        inverse = lax.rsqrt(spread + 1e-05)
        normed = centered * inverse
        out_ref[span, :] = (normed * gain).astype(BF)
        scaled = u_ref[span, :].astype(F32) * gain
        first = jnp.mean(scaled, axis=-1, keepdims=True)
        second = jnp.mean(scaled * normed, axis=-1, keepdims=True)
        gradient = inverse * (scaled - first - normed * second)
        res[span, :] = gradient
        rlow[span, :] = gradient.astype(BF)
        return carry

    lax.fori_loop(0, 2 * SEG // block, norm, 0, unroll=2)
    layer_out = pltpu.make_async_copy(out_ref, out_hbm, sems.at[34])
    layer_out.start()

    for i in range(pairs):
        rlow_t[128 * i : 128 * (i + 1), :] = rlow[:, 128 * i : 128 * (i + 1)].T

    def partial_of(j, carry):
        both = jnp.concatenate([mixed[2 * j], mixed[2 * j + 1]], axis=1)
        product = jnp.dot(rlow_t[...], both, preferred_element_type=F32).astype(BF)
        part[j, 0] = product[:, :128].reshape(Y, Z, rows, 128)
        part[j, 1] = product[:, 128:].reshape(Y, Z, rows, 128)
        return carry

    def pair_send(j):
        on_core(lambda c: send(part.at[j, 1 - c], r0.at[j], sems.at[20], sems.at[21], partner))

    for j in range(X):
        partial_of(j, 0)
        if j > 0:
            pair_send(j - 1)
    pair_send(X - 1)

    tall = 2 if Y % 2 == 0 and Z * rows == 128 else 1
    height = tall * Z * rows

    def rows_of(ref, i, width):
        start = i * tall
        return jnp.concatenate(
            [
                ref[j, c, pl.ds(start, tall)].reshape(height, width)
                for j in range(X)
                for c in (0, 1)
            ],
            axis=1,
        )

    def mix_back(i, carry):
        product = lax.dot_general(rlow[...], rows_of(go, i, 128), NT, preferred_element_type=F32).astype(BF)
        for k in range(height // 128):
            mgrad[(height // 128) * i + k] = product[:, 128 * k : 128 * (k + 1)]
        return carry

    lax.fori_loop(0, Y // tall, mix_back, 0)

    settle(r0, sems.at[21])

    def pair_sum(i, carry):
        j, k = i // Y, i % Y
        a1[j, k] = (part[j, core, k].astype(F32) + r0[j, k].astype(F32)).astype(BF)
        return carry

    lax.fori_loop(0, X * Y, pair_sum, 0)

    def reduce_first(c):
        n, f = first_axis(c)
        far = (f + n // 2) % n
        kept = pltpu.make_async_copy(a1.at[(x,) + yz(c, far, every)], tie_in.at[x], sems.at[1])
        kept.start()
        for t in range(1, X):
            k = (x + t) % X
            send(a1.at[(k,) + yz(c, far, every)], tie_in.at[x], sems.at[30], sems.at[31], at_x(c, k))
        own = pltpu.make_async_copy(a1.at[(every,) + yz(c, f, every)], r1.at[0], sems.at[0])
        own.start()
        for t in far_first(n):
            if 2 * t != n:
                g = (f + t) % n
                send(a1.at[(every,) + yz(c, g, every)], r1.at[t], sems.at[22], sems.at[23], at_first(c, g))
        own.wait()
        kept.wait()

    on_core(reduce_first)

    def attend_back(it, carry):
        p, s = it // 2, it % 2
        span = pl.ds(pl.multiple_of(s * SEG, SEG), SEG)
        keys, values = joint[pairs + p, span, :], joint[2 * pairs + p, span, :]
        outer = apart(mgrad[p, span, :])
        shares = shares_buf[it]
        shares_grad = lax.dot_general(outer, values, NT, preferred_element_type=F32)
        inner = jnp.sum(shares_grad * shares, axis=-1, keepdims=True)
        scores_grad = (shares * (shares_grad - inner) * scale).astype(BF)
        query_grad = jnp.dot(scores_grad, keys, preferred_element_type=F32)
        jgrad[p, span, :] = joined(query_grad).astype(BF)
        key_grad = jnp.dot(scores_grad.T, apart(joint[p, span, :]), preferred_element_type=F32)
        jgrad[pairs + p, span, :] = key_grad.astype(BF)
        value_grad = jnp.dot(shares.astype(BF).T, outer, preferred_element_type=F32)
        jgrad[2 * pairs + p, span, :] = value_grad.astype(BF)
        return carry

    lax.fori_loop(0, pairs, attend_back, 0, unroll=4)

    if X > 1:
        settle(tie_in.at[pl.ds(0, X - 1)], sems.at[31])
    far_total = tie_in[0].astype(F32)
    for k in range(1, X):
        far_total = far_total + tie_in[k].astype(F32)
    tie_sum[...] = far_total.astype(BF)


    def far_send(c):
        n, f = first_axis(c)
        send(tie_sum, tie_got, sems.at[32], sems.at[33], at_first(c, (f + n // 2) % n))

    on_core(far_send)

    lax.fori_loop(pairs, 2 * pairs, attend_back, 0, unroll=4)

    def input_back(i, carry):
        left = jnp.concatenate([jgrad[g] for g in range(3 * pairs)], axis=1)
        product = lax.dot_general(left, rows_of(gj, i, wide), NT, preferred_element_type=F32)
        span = pl.ds(pl.multiple_of(i * height, height), height)
        grad_ref[:, span] = (res[:, span] + product).astype(BF)
        return carry

    lax.fori_loop(0, Y // tall, input_back, 0)

    gradient_out = pltpu.make_async_copy(grad_ref, grad_hbm, sems.at[35])
    gradient_out.start()

    def headers_all(c):
        m, s = second_axis(c)
        settle(panel.at[yz(c, every, pl.ds(0, m - 1))], sems.at[19])

    on_core(headers_all)

    sub = lax.broadcasted_iota(jnp.int32, (pairs, 128), 0)
    low = lax.broadcasted_iota(jnp.int32, (pairs, 128), 1) < HD
    head = 2 * sub + jnp.where(low, 0, 1)
    slopes = jnp.zeros((pairs, 128), F32)
    for h in range(2 * pairs):
        slopes = jnp.where(head == h, 2.0 ** (-(h + 1.0) * 4.0 / (2 * pairs)), slopes)
    for i in range(2):
        own_depth = depth_ref[ctx * 2 + i]
        scores, values = [], []
        for l in range(lists_ref.shape[1] + 1):
            if l == lists_ref.shape[1]:
                tile = panel[y, z, i]
                depth = own_depth
            else:
                listed = lists_ref[i, l]
                other = jnp.maximum(listed, 0)
                tile = panel[other // (2 * Z), (other // 2) % Z, other % 2]
                depth = depth_ref[other]
            product = hq[i] * tile[:pairs].astype(F32)
            score = jnp.where(
                low,
                jnp.sum(jnp.where(low, product, 0.0), axis=-1, keepdims=True),
                jnp.sum(jnp.where(low, 0.0, product), axis=-1, keepdims=True),
            )
            score = score * scale - slopes * (own_depth - depth).astype(F32)
            if l < lists_ref.shape[1]:
                score = jnp.where(listed >= 0, score, -1e30)
            scores.append(score)
            values.append(tile[pairs:].astype(F32))
        top = functools.reduce(jnp.maximum, scores)
        raised = [jnp.exp(v - top) for v in scores]
        below = 1.0 / functools.reduce(jnp.add, raised)
        context = functools.reduce(
            jnp.add, [(r * below).astype(BF).astype(F32) * v for r, v in zip(raised, values)]
        )
        for p in range(pairs):
            wide_context[i : i + 1, 128 * p : 128 * (p + 1)] = context[p : p + 1]
    context_ref[...] = wide_context[...].astype(BF)

    if Y > 2:
        settle(r1.at[pl.ds(0, Y - 2)], sems.at[23])
    settle(tie_got, sems.at[33])

    def first_sum(j, carry):
        total = r1[0, j].astype(F32)
        for k in range(1, Y):
            if 2 * k != Y:
                total = total + r1[k, j].astype(F32)
        a2[j] = total
        return carry

    lax.fori_loop(0, X, first_sum, 0)
    a2[x] = a2[x] + tie_got[...].astype(F32)
    a2_low[...] = a2[...].astype(BF)

    def reduce_second(c):
        m, s = second_axis(c)
        own = pltpu.make_async_copy(a2_low.at[:, s], r2.at[0], sems.at[0])
        own.start()
        for t in far_first(m):
            g = (s + t) % m
            send(a2_low.at[:, g], r2.at[t], sems.at[24], sems.at[25], at_second(c, g))
        own.wait()

    on_core(reduce_second)
    settle(r2.at[pl.ds(0, Y - 1)], sems.at[25])
    total = r2[0].astype(F32)
    for k in range(1, Y):
        total = total + r2[k].astype(F32)
    a3[...] = total

    own = pltpu.make_async_copy(a3.at[x], r3.at[x], sems.at[0])
    own.start()
    for t in range(1, X):
        k = (x + t) % X
        send(a3.at[k], r3.at[x], sems.at[26], sems.at[27], (k * 2 + core, ctx))
    own.wait()
    if X > 1:
        settle(r3.at[pl.ds(0, X - 1)], sems.at[27])
    final = r3[0]
    for k in range(1, X):
        final = final + r3[k]
    dw_ref[...] = final
    layer_out.wait()
    gradient_out.wait()

    def drain(c):
        n, f = first_axis(c)
        m, s = second_axis(c)
        if X > 1:
            settle(gj.at[pl.ds(0, X - 1), c, y, z], sems.at[2])
            settle(go.at[pl.ds(0, min(X - 1, 2)), c], sems.at[12])
            if X == 4:
                settle(go.at[x, c], sems.at[13])
            settle(r3.at[pl.ds(0, X - 1)], sems.at[26])
            settle(tie_in.at[pl.ds(0, X - 1)], sems.at[30])
        settle(go.at[(x, c) + yz(c, pl.ds(0, n - 1), s)], sems.at[4])
        settle(gj.at[:, c], sems.at[10])
        settle(go.at[:, c], sems.at[14])
        settle(panel.at[yz(c, pl.ds(0, n - 1), s)], sems.at[16])
        settle(r0, sems.at[20])
        if n > 2:
            settle(r1.at[pl.ds(0, n - 2)], sems.at[22])
        settle(r2.at[pl.ds(0, m - 1)], sems.at[24])
        settle(tie_sum, sems.at[32])
        settle(gj.at[(every, c) + yz(c, pl.ds(0, n - 1), s)], sems.at[6])
        settle(gj.at[(every, c) + yz(c, every, pl.ds(0, m - 1))], sems.at[7])
        settle(go.at[(x, c) + yz(c, every, pl.ds(0, m - 1))], sems.at[8])
        settle(panel.at[yz(c, every, pl.ds(0, m - 1))], sems.at[18])

    on_core(drain)


def call_layer(dims, tokens, upstream, joint_weight, output_weight, gain, lists, depth):
    X, Y, Z = dims
    T, D = tokens.shape
    pairs = D // 128
    rows, wide = joint_weight.shape
    vmem = pl.BlockSpec(memory_space=pltpu.VMEM)
    anywhere = pl.BlockSpec(memory_space=pl.ANY)
    V = pltpu.VMEM
    dma = pltpu.SemaphoreType.DMA
    most = max(Y, Z)
    return pl.pallas_call(
        functools.partial(layer_kernel, dims),
        out_shape=(
            jax.ShapeDtypeStruct((T, D), BF),
            jax.ShapeDtypeStruct((T, D), BF),
            jax.ShapeDtypeStruct((rows, 128), F32),
            jax.ShapeDtypeStruct((2, D), BF),
        ),
        in_specs=[anywhere] * 7,
        out_specs=(anywhere, anywhere, vmem, vmem),
        scratch_shapes=[
            V((T, D), BF),
            V((T, D), BF),
            V((T, D), BF),
            V((T, D), BF),
            V((Y, Z, 2, 2 * pairs, 128), BF),
            V((X, 2, Y, Z, rows, wide), BF),
            V((X, 2, Y, Z, rows, 128), BF),
            V((3 * pairs, T, 128), BF),
            V((2 * pairs, 2 * SEG, SEG), F32),
            V((pairs, T, 128), BF),
            V((T, D), F32),
            V((T, D), BF),
            V((D, T), BF),
            V((X, 2, Y, Z, rows, 128), BF),
            V((X, Y, Z, rows, 128), BF),
            V((X, Y, Z, rows, 128), BF),
            V((Y, X, Z, rows, 128), BF),
            V((X, Z, rows, 128), BF),
            V((Z, rows, 128), BF),
            V((Z, rows, 128), BF),
            V((X, Z, rows, 128), F32),
            V((X, Z, rows, 128), BF),
            V((Y, X, rows, 128), BF),
            V((X, rows, 128), F32),
            V((X, rows, 128), F32),
            V((pairs, T, 128), BF),
            V((3 * pairs, T, 128), BF),
            V((2, pairs, 128), F32),
            V((2, 2 * pairs, 128), F32),
            V((2, 2 * pairs, 128), BF),
            V((2, D), F32),
            dma((most,)),
            dma((2, most // 2, most)),
            dma((2, most // 2)),
            dma((2, 2)),
            V(gain.shape, BF),
            pltpu.SMEM(lists.shape, jnp.int32),
            pltpu.SMEM(depth.shape, jnp.int32),
            dma((39,)),
        ],
        compiler_params=pltpu.CompilerParams(collective_id=0, has_side_effects=True),
        name="segment_layer",
    )(tokens, upstream, joint_weight, output_weight, gain, lists, depth)


def on_device(
    dims, segment_tokens, upstream_grad, joint_weight, output_weight, norm_gain, ancestors, outline_depth
):
    T, D = segment_tokens.shape[1:]
    layer_output, input_gradient, weight_gradient, context = call_layer(
        dims,
        segment_tokens[0],
        upstream_grad[0],
        joint_weight,
        output_weight,
        norm_gain.reshape(D // 128, 128),
        ancestors[0],
        outline_depth[0],
    )
    return (layer_output[None], input_gradient[None], weight_gradient.T, context[None])


def solution(mesh, dims=TORUS):
    return jax.shard_map(
        functools.partial(on_device, dims),
        mesh=mesh,
        in_specs=(
            P("dp", "ctx", None),
            P("dp", "ctx", None),
            P("ctx", "dp"),
            P("ctx", "dp"),
            P(),
            P("dp", "ctx", None),
            P("dp", None),
        ),
        out_specs=(
            P("dp", "ctx", None),
            P("dp", "ctx", None),
            P("dp", "ctx"),
            P("dp", "ctx", None),
        ),
        check_vma=False,
    )
```

time: 105 us -> 88.9 us (0.85); the launches traced: 105 us -> 87.4 us
  Pallas kernels: 95.4 us -> 82.7 us
  local copies, waits for them, and re-layouts: 7.7 us -> 4 us
    pallas_call x1, Pallas kernels: 95.4 us -> 82.7 us  [call_layer(): pl.pallas_call(functools.partial(layer_kernel, dims), out_shape=(jax.Shap...]
    reshape x2 -> x0, local copies, waits for them, and re-layouts: 2.25 us -> none  [the longest x1 1.65 us: on_device(): panel_heads = panel.reshape(total_segments, 2, H, HD)]
    unnamed x19 -> x10, local copies, waits for them, and re-layouts: 4.41 us -> 4 us
where the time goes in v2:
time: 88.9 us; the launch traced here: 87.4 us
  Pallas kernels  82.7 us (93%)
  local copies, waits for them, and re-layouts  4 us (4%)
    pallas_call x1, Pallas kernels, call_layer(): pl.pallas_call(functools.partial(layer_kernel, dims), out_shape=(jax.Shap...  82.7 us
    unnamed x10, local copies, waits for them, and re-layouts  4 us

profile of v2, /device:TPU:1, one launch (start us, length us, event | category | flops | bytes accessed | tf_op | source)
XLA Modules:
  0.0 87.4 jit_solution(15119591431856609455)
XLA Ops:
  0.6 82.7 %segment_layer.1 = (bf16[256,1024]{1,0:T(8,128)(2,1)}, bf16[256,1024]{1,0:T(8,128)(2,1)}, f32[16,128]{1,0:T(8,128)}, bf16[2,1024]{1,0:T(2,128)(2,1)}) custom-call(bf16[256,1024]{1,0:T(8,128)(2,1)} %bitcast.9, bf16[256,1024]{1,0:T(8,128)(2,1)} %bitcast.10, bf16[16,384]{1,0:T(8,128)(2,1)} %wj_ref.1, bf16[16,128]{1,0:T(8,128)(2,1)} %wo_ref.1, ...), custom_call_target="tpu_custom_call" | custom-call | tf_op jit(solution)/shard_map/segment_layer/pallas_call | solution.py:615
  83.4 0.0 copy-start
  83.4 1.9 %copy.15 = bf16[1,256,1024]{2,1,0:T(8,128)(2,1)} copy(bf16[1,256,1024]{2,1,0:T(8,128)(2,1)} %bitcast.12) | data formatting | bytes 1048576
  85.3 0.0 copy-done
  85.3 0.0 copy-start.1
  85.3 0.8 copy.16
  86.1 0.0 copy-done.1
  86.1 0.0 copy-start.2
  86.1 0.6 copy.17
  86.7 0.1 copy-done.2
  86.8 0.6 copy.18
Async XLA Ops:
  83.4 1.9 %copy-start = (bf16[256,1024]{1,0:T(8,128)(2,1)S(1)}, bf16[256,1024]{1,0:T(8,128)(2,1)}, u32[]{:S(2)}) copy-start(bf16[256,1024]{1,0:T(8,128)(2,1)} %get-tuple-element.9) | copy-start | bytes 1572868
  85.3 0.8 copy-start.1
  86.1 0.7 copy-start.2

commit v3 on v2

--- a/solution.py
+++ b/solution.py
@@ -56,8 +56,6 @@
     a2,
     a2_low,
     r2,
-    a3,
-    r3,
     mgrad,
     jgrad,
     hq,
@@ -140,7 +138,16 @@
     for t in range(1, Z):
         pl.semaphore_signal(barrier, device_id=(dp, y * Z + (z + t) % Z), device_id_type=MESH)
     pl.semaphore_signal(barrier, device_id=partner, device_id_type=MESH)
-    pl.semaphore_wait(barrier, X + Y + Z - 2)
+
+    def greet(c):
+        m, s = second_axis(c)
+        for a in range(1, X):
+            for t in range(1, m):
+                peer = ((x + a) % X * 2 + c, at_second(c, (s + t) % m)[1])
+                pl.semaphore_signal(barrier, device_id=peer, device_id_type=MESH)
+
+    on_core(greet)
+    pl.semaphore_wait(barrier, X + Y + Z - 2 + (X - 1) * (Y - 1))
 
     def gather(c):
         n, f = first_axis(c)
@@ -546,31 +553,22 @@
 
     def reduce_second(c):
         m, s = second_axis(c)
-        own = pltpu.make_async_copy(a2_low.at[:, s], r2.at[0], sems.at[0])
-        own.start()
-        for t in far_first(m):
-            g = (s + t) % m
-            send(a2_low.at[:, g], r2.at[t], sems.at[24], sems.at[25], at_second(c, g))
-        own.wait()
+        for t in [*far_first(m), 0]:
+            for a in range(X - 1, -1, -1):
+                k, g = (x + a) % X, (s + t) % m
+                if a == 0 and t == 0:
+                    own = pltpu.make_async_copy(a2_low.at[k, g], r2.at[0], sems.at[0])
+                    own.start()
+                    own.wait()
+                else:
+                    peer = (k * 2 + c, at_second(c, g)[1])
+                    send(a2_low.at[k, g], r2.at[a * m + t], sems.at[24], sems.at[25], peer)
 
     on_core(reduce_second)
-    settle(r2.at[pl.ds(0, Y - 1)], sems.at[25])
-    total = r2[0].astype(F32)
-    for k in range(1, Y):
-        total = total + r2[k].astype(F32)
-    a3[...] = total
-
-    own = pltpu.make_async_copy(a3.at[x], r3.at[x], sems.at[0])
-    own.start()
-    for t in range(1, X):
-        k = (x + t) % X
-        send(a3.at[k], r3.at[x], sems.at[26], sems.at[27], (k * 2 + core, ctx))
-    own.wait()
-    if X > 1:
-        settle(r3.at[pl.ds(0, X - 1)], sems.at[27])
-    final = r3[0]
-    for k in range(1, X):
-        final = final + r3[k]
+    settle(r2.at[pl.ds(1, X * Y - 1)], sems.at[25])
+    final = r2[0].astype(F32)
+    for k in range(1, X * Y):
+        final = final + r2[k].astype(F32)
     dw_ref[...] = final
     layer_out.wait()
     gradient_out.wait()
@@ -583,7 +581,6 @@
             settle(go.at[pl.ds(0, min(X - 1, 2)), c], sems.at[12])
             if X == 4:
                 settle(go.at[x, c], sems.at[13])
-            settle(r3.at[pl.ds(0, X - 1)], sems.at[26])
             settle(tie_in.at[pl.ds(0, X - 1)], sems.at[30])
         settle(go.at[(x, c) + yz(c, pl.ds(0, n - 1), s)], sems.at[4])
         settle(gj.at[:, c], sems.at[10])
@@ -592,7 +589,7 @@
         settle(r0, sems.at[20])
         if n > 2:
             settle(r1.at[pl.ds(0, n - 2)], sems.at[22])
-        settle(r2.at[pl.ds(0, m - 1)], sems.at[24])
+        settle(r2.at[pl.ds(1, X * m - 1)], sems.at[24])
         settle(tie_sum, sems.at[32])
         settle(gj.at[(every, c) + yz(c, pl.ds(0, n - 1), s)], sems.at[6])
         settle(gj.at[(every, c) + yz(c, every, pl.ds(0, m - 1))], sems.at[7])
@@ -645,9 +642,7 @@
             V((Z, rows, 128), BF),
             V((X, Z, rows, 128), F32),
             V((X, Z, rows, 128), BF),
-            V((Y, X, rows, 128), BF),
-            V((X, rows, 128), F32),
-            V((X, rows, 128), F32),
+            V((X * Y, rows, 128), BF),
             V((pairs, T, 128), BF),
             V((3 * pairs, T, 128), BF),
             V((2, pairs, 128), F32),
@@ -668,6 +663,33 @@
     )(tokens, upstream, joint_weight, output_weight, gain, lists, depth)
 
 
+def finish_kernel(*refs):
+    count = len(refs) // 3
+    sources, targets, held, sems = refs[:count], refs[count : 2 * count], refs[2 * count : 3 * count], refs[-1]
+    arrive = [pltpu.make_async_copy(a, h, sems.at[0, i]) for i, (a, h) in enumerate(zip(sources, held))]
+    leave = [pltpu.make_async_copy(h, b, sems.at[1, i]) for i, (h, b) in enumerate(zip(held, targets))]
+    for copy in arrive:
+        copy.start()
+    for first, second in zip(arrive, leave):
+        first.wait()
+        second.start()
+    for copy in leave:
+        copy.wait()
+
+
+def finish(*arrays):
+    anywhere = pl.BlockSpec(memory_space=pl.ANY)
+    return pl.pallas_call(
+        finish_kernel,
+        out_shape=tuple(jax.ShapeDtypeStruct(a.shape, a.dtype) for a in arrays),
+        in_specs=[anywhere] * len(arrays),
+        out_specs=(anywhere,) * len(arrays),
+        scratch_shapes=[pltpu.VMEM(a.shape, a.dtype) for a in arrays]
+        + [pltpu.SemaphoreType.DMA((2, len(arrays)))],
+        name="hand_on",
+    )(*arrays)
+
+
 def on_device(
     dims, segment_tokens, upstream_grad, joint_weight, output_weight, norm_gain, ancestors, outline_depth
 ):
@@ -681,6 +703,9 @@
         norm_gain.reshape(D // 128, 128),
         ancestors[0],
         outline_depth[0],
+    )
+    layer_output, input_gradient, weight_gradient, context = finish(
+        layer_output, input_gradient, weight_gradient, context
     )
     return (layer_output[None], input_gradient[None], weight_gradient.T, context[None])
 

time: 88.9 us -> 86.3 us (0.971); the launches traced: 87.4 us -> 85.8 us
  local copies, waits for them, and re-layouts: 4 us -> 0 us
  Pallas kernels: 82.7 us -> 85.1 us
    unnamed x10 -> x0, local copies, waits for them, and re-layouts: 4 us -> none
    pallas_call x0 -> x1, Pallas kernels: none -> 2.08 us  [finish(): pl.pallas_call(finish_kernel, out_shape=tuple((jax.ShapeDtypeStruct(a.sha...]
where the time goes in v3:
time: 86.3 us; the launch traced here: 85.8 us
  Pallas kernels  85.1 us (99%)
    pallas_call x1, Pallas kernels, call_layer(): pl.pallas_call(functools.partial(layer_kernel, dims), out_shape=(jax.Shap...  83.1 us
    pallas_call x1, Pallas kernels, finish(): pl.pallas_call(finish_kernel, out_shape=tuple((jax.ShapeDtypeStruct(a.sha...  2.08 us

profile of v3, /device:TPU:1, one launch (start us, length us, event | category | flops | bytes accessed | tf_op | source)
XLA Modules:
  0.0 85.8 jit_solution(6145180912096362226)
XLA Ops:
  0.6 83.1 %segment_layer.1 = (bf16[256,1024]{1,0:T(8,128)(2,1)}, bf16[256,1024]{1,0:T(8,128)(2,1)}, f32[16,128]{1,0:T(8,128)}, bf16[2,1024]{1,0:T(2,128)(2,1)}) custom-call(bf16[256,1024]{1,0:T(8,128)(2,1)} %bitcast.9, bf16[256,1024]{1,0:T(8,128)(2,1)} %bitcast.10, bf16[16,384]{1,0:T(8,128)(2,1)} %wj_ref.1, bf16[16,128]{1,0:T(8,128)(2,1)} %wo_ref.1, ...), custom_call_target="tpu_custom_call" | custom-call | tf_op jit(solution)/shard_map/segment_layer/pallas_call | solution.py:612
  83.7 2.1 %hand_on.1 = (bf16[256,1024]{1,0:T(8,128)(2,1)}, bf16[256,1024]{1,0:T(8,128)(2,1)}, f32[16,128]{1,0:T(8,128)}, bf16[2,1024]{1,0:T(2,128)(2,1)}) custom-call(bf16[256,1024]{1,0:T(8,128)(2,1)} %get-tuple-element.12.refs_0_, bf16[256,1024]{1,0:T(8,128)(2,1)} %get-tuple-element.13.refs_1_, f32[16,128]{1,0:T(8,128)} %get-tuple-element.14.refs_2_, ...), custom_call_target="tpu_custom_call" | custom-call | tf_op jit(solution)/shard_map/hand_on/pallas_call | solution.py:682

commit v4 on v3

--- a/solution.py
+++ b/solution.py
@@ -29,14 +29,12 @@
     gain_hbm,
     lists_hbm,
     depth_hbm,
-    out_hbm,
-    grad_hbm,
+    out_ref,
+    grad_ref,
     dw_ref,
     context_ref,
     x_ref,
     u_ref,
-    out_ref,
-    grad_ref,
     panel,
     gj,
     go,
@@ -309,7 +307,7 @@
         mixed[p, span, :] = joined(both).astype(BF)
         return carry
 
-    lax.fori_loop(0, pairs, attend, 0, unroll=4)
+    lax.fori_loop(0, pairs, attend, 0, unroll=8)
 
     def hand_output_weights(c):
         if X == 4:
@@ -319,7 +317,7 @@
 
     on_core(hand_output_weights)
 
-    lax.fori_loop(pairs, 2 * pairs, attend, 0, unroll=4)
+    lax.fori_loop(pairs, 2 * pairs, attend, 0, unroll=8)
 
 
     settle_out = lambda c: settle(go.at[:, 1 - c], sems.at[15])
@@ -370,9 +368,7 @@
         rlow[span, :] = gradient.astype(BF)
         return carry
 
-    lax.fori_loop(0, 2 * SEG // block, norm, 0, unroll=2)
-    layer_out = pltpu.make_async_copy(out_ref, out_hbm, sems.at[34])
-    layer_out.start()
+    lax.fori_loop(0, 2 * SEG // block, norm, 0, unroll=4)
 
     for i in range(pairs):
         rlow_t[128 * i : 128 * (i + 1), :] = rlow[:, 128 * i : 128 * (i + 1)].T
@@ -460,7 +456,7 @@
         jgrad[2 * pairs + p, span, :] = value_grad.astype(BF)
         return carry
 
-    lax.fori_loop(0, pairs, attend_back, 0, unroll=4)
+    lax.fori_loop(0, pairs, attend_back, 0, unroll=8)
 
     if X > 1:
         settle(tie_in.at[pl.ds(0, X - 1)], sems.at[31])
@@ -476,7 +472,7 @@
 
     on_core(far_send)
 
-    lax.fori_loop(pairs, 2 * pairs, attend_back, 0, unroll=4)
+    lax.fori_loop(pairs, 2 * pairs, attend_back, 0, unroll=8)
 
     def input_back(i, carry):
         left = jnp.concatenate([jgrad[g] for g in range(3 * pairs)], axis=1)
@@ -487,8 +483,6 @@
 
     lax.fori_loop(0, Y // tall, input_back, 0)
 
-    gradient_out = pltpu.make_async_copy(grad_ref, grad_hbm, sems.at[35])
-    gradient_out.start()
 
     def headers_all(c):
         m, s = second_axis(c)
@@ -570,8 +564,6 @@
     for k in range(1, X * Y):
         final = final + r2[k].astype(F32)
     dw_ref[...] = final
-    layer_out.wait()
-    gradient_out.wait()
 
     def drain(c):
         n, f = first_axis(c)
@@ -612,16 +604,14 @@
     return pl.pallas_call(
         functools.partial(layer_kernel, dims),
         out_shape=(
-            jax.ShapeDtypeStruct((T, D), BF),
-            jax.ShapeDtypeStruct((T, D), BF),
-            jax.ShapeDtypeStruct((rows, 128), F32),
-            jax.ShapeDtypeStruct((2, D), BF),
+            V((T, D), BF),
+            V((T, D), BF),
+            V((rows, 128), F32),
+            V((2, D), BF),
         ),
         in_specs=[anywhere] * 7,
-        out_specs=(anywhere, anywhere, vmem, vmem),
+        out_specs=(vmem,) * 4,
         scratch_shapes=[
-            V((T, D), BF),
-            V((T, D), BF),
             V((T, D), BF),
             V((T, D), BF),
             V((Y, Z, 2, 2 * pairs, 128), BF),
@@ -664,16 +654,14 @@
 
 
 def finish_kernel(*refs):
-    count = len(refs) // 3
-    sources, targets, held, sems = refs[:count], refs[count : 2 * count], refs[2 * count : 3 * count], refs[-1]
-    arrive = [pltpu.make_async_copy(a, h, sems.at[0, i]) for i, (a, h) in enumerate(zip(sources, held))]
-    leave = [pltpu.make_async_copy(h, b, sems.at[1, i]) for i, (h, b) in enumerate(zip(held, targets))]
-    for copy in arrive:
+    count = len(refs) // 2
+    copies = [
+        pltpu.make_async_copy(a, b, refs[-1].at[i])
+        for i, (a, b) in enumerate(zip(refs[:count], refs[count : 2 * count]))
+    ]
+    for copy in copies:
         copy.start()
-    for first, second in zip(arrive, leave):
-        first.wait()
-        second.start()
-    for copy in leave:
+    for copy in copies:
         copy.wait()
 
 
@@ -684,8 +672,8 @@
         out_shape=tuple(jax.ShapeDtypeStruct(a.shape, a.dtype) for a in arrays),
         in_specs=[anywhere] * len(arrays),
         out_specs=(anywhere,) * len(arrays),
-        scratch_shapes=[pltpu.VMEM(a.shape, a.dtype) for a in arrays]
-        + [pltpu.SemaphoreType.DMA((2, len(arrays)))],
+        compiler_params=pltpu.CompilerParams(vmem_limit_bytes=1 << 20),
+        scratch_shapes=[pltpu.SemaphoreType.DMA((len(arrays),))],
         name="hand_on",
     )(*arrays)
 

time: 86.3 us -> 84.5 us (0.979)
  Pallas kernels: 85.1 us -> 83.4 us
    pallas_call x1, Pallas kernels: 2.08 us -> 1.01 us  [finish(): pl.pallas_call(finish_kernel, out_shape=tuple((jax.ShapeDtypeStruct(a.sha...]
where the time goes in v4:
time: 84.5 us; the launch traced here: 84 us
  Pallas kernels  83.4 us (99%)
    pallas_call x1, Pallas kernels, call_layer(): pl.pallas_call(functools.partial(layer_kernel, dims), out_shape=(V((T, D)...  82.4 us

profile of v4, /device:TPU:1, one launch (start us, length us, event | category | flops | bytes accessed | tf_op | source)
XLA Modules:
  0.0 84.0 jit_solution(12087886057511036773)
XLA Ops:
  0.6 82.4 %segment_layer.1 = (bf16[256,1024]{1,0:T(8,128)(2,1)S(1)}, bf16[256,1024]{1,0:T(8,128)(2,1)S(1)}, f32[16,128]{1,0:T(8,128)S(1)}, bf16[2,1024]{1,0:T(2,128)(2,1)S(1)}) custom-call(bf16[256,1024]{1,0:T(8,128)(2,1)} %bitcast.9, bf16[256,1024]{1,0:T(8,128)(2,1)} %bitcast.10, bf16[16,384]{1,0:T(8,128)(2,1)} %wj_ref.1, bf16[16,128]{1,0:T(8,128)(2,1)} %wo_ref.1, ...), custom_call_target="tpu_custom_call" | custom-call | tf_op jit(solution)/shard_map/segment_layer/pallas_call | solution.py:604
  83.0 1.0 %hand_on.1 = (bf16[256,1024]{1,0:T(8,128)(2,1)}, bf16[256,1024]{1,0:T(8,128)(2,1)}, f32[16,128]{1,0:T(8,128)}, bf16[2,1024]{1,0:T(2,128)(2,1)}) custom-call(bf16[256,1024]{1,0:T(8,128)(2,1)S(1)} %get-tuple-element.12.refs_0_, bf16[256,1024]{1,0:T(8,128)(2,1)S(1)} %get-tuple-element.13.refs_1_, f32[16,128]{1,0:T(8,128)S(1)} %get-tuple-element.14.refs_2_, ...), custom_call_target="tpu_custom_call" | custom-call | tf_op jit(solution)/shard_map/hand_on/pallas_call | solution.py:670

commit v5 on v4

--- a/solution.py
+++ b/solution.py
@@ -381,7 +381,7 @@
         return carry
 
     def pair_send(j):
-        on_core(lambda c: send(part.at[j, 1 - c], r0.at[j], sems.at[20], sems.at[21], partner))
+        on_core(lambda c: send(part.at[j, 1 - c], r0.at[j], sems.at[20], sems.at[21 if 2 * j < X else 26], partner))
 
     for j in range(X):
         partial_of(j, 0)
@@ -411,14 +411,35 @@
 
     lax.fori_loop(0, Y // tall, mix_back, 0)
 
-    settle(r0, sems.at[21])
-
     def pair_sum(i, carry):
         j, k = i // Y, i % Y
         a1[j, k] = (part[j, core, k].astype(F32) + r0[j, k].astype(F32)).astype(BF)
         return carry
 
-    lax.fori_loop(0, X * Y, pair_sum, 0)
+    halves = [(0, X)] if X == 1 else [(0, X // 2), (X // 2, X)]
+
+    def near_send(first, last):
+        def body(c):
+            n, f = first_axis(c)
+            for t in far_first(n):
+                if 2 * t != n:
+                    g = (f + t) % n
+                    span = pl.ds(first, last - first)
+                    send(
+                        a1.at[(span,) + yz(c, g, every)],
+                        r1.at[t, span],
+                        sems.at[22],
+                        sems.at[23],
+                        at_first(c, g),
+                    )
+
+        on_core(body)
+
+    for which, (first, last) in enumerate(halves):
+        settle(r0.at[pl.ds(first, last - first)], sems.at[(21, 26)[which]])
+        lax.fori_loop(first * Y, last * Y, pair_sum, 0)
+        if which + 1 < len(halves):
+            near_send(first, last)
 
     def reduce_first(c):
         n, f = first_axis(c)
@@ -430,14 +451,11 @@
             send(a1.at[(k,) + yz(c, far, every)], tie_in.at[x], sems.at[30], sems.at[31], at_x(c, k))
         own = pltpu.make_async_copy(a1.at[(every,) + yz(c, f, every)], r1.at[0], sems.at[0])
         own.start()
-        for t in far_first(n):
-            if 2 * t != n:
-                g = (f + t) % n
-                send(a1.at[(every,) + yz(c, g, every)], r1.at[t], sems.at[22], sems.at[23], at_first(c, g))
         own.wait()
         kept.wait()
 
     on_core(reduce_first)
+    near_send(*halves[-1])
 
     def attend_back(it, carry):
         p, s = it // 2, it % 2

time: 84.5 us -> 83.8 us (level)
  no operation moved by 1% of the time
where the time goes in v5:
time: 83.8 us; the launch traced here: 83.6 us
  Pallas kernels  83 us (99%)
    pallas_call x1, Pallas kernels, call_layer(): pl.pallas_call(functools.partial(layer_kernel, dims), out_shape=(V((T, D)...  82 us

profile of v5, /device:TPU:1, one launch (start us, length us, event | category | flops | bytes accessed | tf_op | source)
XLA Modules:
  0.0 83.6 jit_solution(14724163351603848358)
XLA Ops:
  0.6 82.0 %segment_layer.1 = (bf16[256,1024]{1,0:T(8,128)(2,1)S(1)}, bf16[256,1024]{1,0:T(8,128)(2,1)S(1)}, f32[16,128]{1,0:T(8,128)S(1)}, bf16[2,1024]{1,0:T(2,128)(2,1)S(1)}) custom-call(bf16[256,1024]{1,0:T(8,128)(2,1)} %bitcast.9, bf16[256,1024]{1,0:T(8,128)(2,1)} %bitcast.10, bf16[16,384]{1,0:T(8,128)(2,1)} %wj_ref.1, bf16[16,128]{1,0:T(8,128)(2,1)} %wo_ref.1, ...), custom_call_target="tpu_custom_call" | custom-call | tf_op jit(solution)/shard_map/segment_layer/pallas_call | solution.py:622
  82.6 1.0 %hand_on.1 = (bf16[256,1024]{1,0:T(8,128)(2,1)}, bf16[256,1024]{1,0:T(8,128)(2,1)}, f32[16,128]{1,0:T(8,128)}, bf16[2,1024]{1,0:T(2,128)(2,1)}) custom-call(bf16[256,1024]{1,0:T(8,128)(2,1)S(1)} %get-tuple-element.12.refs_0_, bf16[256,1024]{1,0:T(8,128)(2,1)S(1)} %get-tuple-element.13.refs_1_, f32[16,128]{1,0:T(8,128)S(1)} %get-tuple-element.14.refs_2_, ...), custom_call_target="tpu_custom_call" | custom-call | tf_op jit(solution)/shard_map/hand_on/pallas_call | solution.py:688
